TPU v7x, 32 devices: a whole 2x2x4 slice. The times are simulated.
32 devices in a mesh: segment: 2 (over core), expert: 16 (over z, y, x).
Axes of the slice: x: 2, y: 2, z: 4, core: 2. Of those that a mesh axis runs over, the one named last changes fastest.
Arguments:
- fwd_tokens: bfloat16 [2, 1024, 2048], P('segment', 'expert'), may hold values from -6 to 6
- fwd_routes: int32 [2, 1024, 8], P('segment', 'expert'), may hold values from 0 to 15, all different within a row; in each aligned block of 64 rows (0 to 63, 64 to 127, ..., all dimensions but the last counted through in order) at most 48 rows name the same one
- fwd_gates: bfloat16 [2, 1024, 8], P('segment', 'expert'), may hold values from 0.049804688 to 0.5
- bwd_tokens: bfloat16 [2, 1024, 2048], P('segment', 'expert'), may hold values from -6 to 6
- bwd_routes: int32 [2, 1024, 8], P('segment', 'expert'), may hold values from 0 to 15, all different within a row; in each aligned block of 64 rows (0 to 63, 64 to 127, ..., all dimensions but the last counted through in order) at most 48 rows name the same one
- bwd_gates: bfloat16 [2, 1024, 8], P('segment', 'expert'), may hold values from 0.049804688 to 0.5
- cotangent: bfloat16 [2, 1024, 2048], P('segment', 'expert'), may hold values from -6 to 6
- w_gate_up: bfloat16 [2, 16, 2048, 1536], P('segment', 'expert'), may hold values from -0.125 to 0.125
- w_down: bfloat16 [2, 16, 768, 2048], P('segment', 'expert'), may hold values from -0.21875 to 0.21875
Outputs:
- forward_out: bfloat16 [2, 1024, 2048], P('segment', 'expert')
- input_grad: bfloat16 [2, 1024, 2048], P('segment', 'expert')
- gate_grad: bfloat16 [2, 1024, 8], P('segment', 'expert')
- grad_gate_up: bfloat16 [2, 16, 2048, 1536], P('segment', 'expert')
- grad_down: bfloat16 [2, 16, 768, 2048], P('segment', 'expert')
Inputs may be any that keep to these rules, and one draw needn't show every extreme that they name: `fwd_routes`: each token names 8 different experts; within each aligned block of 64 tokens of one section no expert is named more than 48 times, a bound that some block reaches. `bwd_routes`: each token names 8 different experts; within each aligned block of 64 tokens of one section no expert is named more than 48 times, a bound that some block reaches.
All inputs are finite; a program needn't handle non-finite values.
Results may differ from a plain program's by a relative error of at most 0.015.
Values may be sent and summed in bfloat16 or wider, within the bound.
No kernel may reach another device: no remote copies, remote signals or barrier semaphores. Data moves between devices by JAX's collectives and lax.ppermute only.
A program may use at most 128 MiB of HBM per device.

v0:
```python
import jax
import jax.numpy as jnp
from jax import lax
from jax.experimental import pallas as pl
from jax.experimental.pallas import tpu as pltpu
from jax.sharding import PartitionSpec as P


LANES = 128
F32 = jnp.float32
BF16 = jnp.bfloat16
NT = (((1,), (1,)), ((), ()))
TN = (((0,), (0,)), ((), ()))
VMEM_BYTES = 50 << 20
ANY = pl.BlockSpec(memory_space=pl.ANY)


def after(value, *others):
    return lax.optimization_barrier((value, *others))[0]


def send(array, size, bit):
    return lax.ppermute(array, "expert", [(i, i ^ (1 << bit)) for i in range(size)])


def three_ways(size, count):
    bits = size.bit_length() - 1
    middle = list(range(2, bits - 1))
    small, large = count // 4, 3 * count // 8
    return [
        (0, small, [0, 1, *middle]),
        (small, small + large, [1, *middle, 0]),
        (small + large, count, [*middle, 0, 1]),
    ]


def send_all(arrays, size, parts, step):
    bits = [p[2][step] for p in parts]
    got = [None] * len(arrays)
    for bit in dict.fromkeys(bits):
        which = [i for i, b in enumerate(bits) if b == bit]
        whole = send(jnp.concatenate([arrays[i] for i in which]), size, bit)
        start = 0
        for i in which:
            got[i] = whole[start : start + arrays[i].shape[0]]
            start += arrays[i].shape[0]
    return got


def top_bit(size):
    return size.bit_length() - 2


def spread_rest(kept, size, parts):
    for step in range(len(parts[0][2]) - 1):
        got = send_all(kept, size, parts, step)
        kept = [jnp.concatenate([k, g]) for k, g in zip(kept, got)]
    return kept, send_all(kept, size, parts, -1)


def add(a, b):
    return (a.astype(F32) + b.astype(F32)).astype(BF16)


def merge(kept, got):
    n = kept.shape[0] // 2
    return add(kept[:n], got[:n]), add(kept[n:], got[n:])


def collect_first(kept, away, size, parts, hold):
    got = after(send_all(away, size, parts, -1), *hold)
    return [merge(k, g) for k, g in zip(kept, got)]


def collect_rest(rows, size, parts):
    for step in range(len(parts[0][2]) - 2, -1, -1):
        got = send_all([r[1] for r in rows], size, parts, step)
        rows = [merge(r[0], g) for r, g in zip(rows, got)]
    sections = lax.axis_size("segment")
    cross = lambda flip: [
        (s * size + i, (s ^ 1) * size + (i ^ flip)) for s in range(sections) for i in range(size)
    ]
    own, other = (jnp.concatenate([r[k] for r in rows]) for k in range(2))
    other = lax.ppermute(other, ("segment", "expert"), cross(size // 2))
    own = lax.ppermute(own, ("segment", "expert"), cross(0))
    return own.astype(F32) + other.astype(F32)


def dense_gates(routes, gates, size):
    hit = routes[:, :, None] == jnp.arange(size, dtype=jnp.int32)[None, None, :]
    return jnp.sum(jnp.where(hit, gates[:, :, None].astype(F32), 0.0), axis=1)


def pick(table, at):
    lane = lax.broadcasted_iota(jnp.int32, table.shape, 1)
    return jnp.sum(jnp.where(lane == at, table.astype(F32), 0.0), axis=1, keepdims=True)


def copies_of(pairs, sems, start):
    return [pltpu.make_async_copy(a, b, sems.at[start + i]) for i, (a, b) in enumerate(pairs)]


def begin(made):
    for copy in made:
        copy.start()


def end(made):
    for copy in made:
        copy.wait()


def starts_of(counts):
    return [sum(counts[:i]) for i in range(len(counts))]


def block_start(step, count):
    return step * count if isinstance(step, int) else pl.multiple_of(step * count, 8)


def span(at, count):
    return pl.ds(at if isinstance(at, int) else pl.multiple_of(at, LANES), count)


def row_pairs(pieces, whole, counts, step, at, columns, outward=False):
    pairs = []
    for piece, count, start in zip(pieces, counts, starts_of(counts)):
        outer = piece.at[pl.ds(block_start(step, count), count), span(at, columns)]
        inner = whole.at[pl.ds(start, count)]
        pairs.append((inner, outer) if outward else (outer, inner))
    return pairs


def once(groups, step):
    return pl.when(step == 0) if groups > 1 else lambda run: run()


CHUNKS = 3
PANELS = 4


def weight_copies(wgu_ref, wdn_ref, wgu, wdn, sems, j):
    ff = wdn.shape[0]
    wide = ff // CHUNKS
    pairs = [(wgu_ref.at[:, span(at, wide)], wgu.at[:, span(at, wide)]) for at in (j * wide, ff + j * wide)]
    rows = span(j * wide, wide)
    pairs.append((wdn_ref.at[rows], wdn.at[rows]))
    return copies_of(pairs, sems, 3 * j)


def back_kernel(counts, groups, me_ref, *refs):
    n = len(counts)
    xd_in, (wgu_ref, wdn_ref) = refs[:n], refs[n : n + 2]
    dx_out, (dh_out, wa_out) = refs[n + 2 : 2 * n + 2], refs[2 * n + 2 : 2 * n + 4]
    x, dy, table, wgu, wdn, dx, extra, dh, wa, gate_grad, sems, w_sems, out_sems = refs[2 * n + 4 :]
    me = me_ref[0]
    step = pl.program_id(0) if groups > 1 else 0
    ff, width = wdn.shape
    lanes = table.shape[1]
    rows = x.shape[0]
    weights = lambda j: weight_copies(wgu_ref, wdn_ref, wgu, wdn, w_sems, j)
    first = once(groups, step)
    ins = copies_of(row_pairs(xd_in, x, counts, step, 0, width), sems, 0)
    dys = copies_of(
        row_pairs(xd_in, dy, counts, step, width, width)
        + row_pairs(xd_in, table, counts, step, 2 * width, lanes),
        sems,
        n,
    )
    begin(ins)
    first(lambda: begin(weights(0)))
    begin(dys)

    @first
    def _():
        for j in range(1, CHUNKS):
            begin(weights(j))

    end(ins)
    end(dys)
    wide = ff // CHUNKS
    gate_grad[...] = jnp.zeros_like(gate_grad)

    @pl.loop(0, CHUNKS)
    def _(j):
        first(lambda: end(weights(j)))
        own = span(j * wide, wide)
        also = span(ff + j * wide, wide)
        gate = jnp.dot(x[...], wgu[:, own], preferred_element_type=F32)
        upper = jnp.dot(x[...], wgu[:, also], preferred_element_type=F32)
        back = lax.dot_general(dy[...], wdn[own], NT, preferred_element_type=F32)
        gate_b = pick(table[...], me)
        sigma = jax.nn.sigmoid(gate)
        silu = gate * sigma
        active = silu * upper
        gate_grad[...] += jnp.sum(active * back, axis=1, keepdims=True)
        wa[:, own] = (active * gate_b).astype(BF16)
        d_active = back * gate_b
        dh[:, own] = (d_active * upper * sigma * (1.0 + gate * (1.0 - sigma))).astype(BF16)
        dh[:, also] = (d_active * silu).astype(BF16)

    lane = lax.broadcasted_iota(jnp.int32, (rows, lanes), 1)
    extra[...] = jnp.where(lane == me, gate_grad[...], 0.0).astype(BF16)
    here = pl.ds(block_start(step, rows), rows)
    outs = copies_of(
        row_pairs(dx_out, extra, counts, step, width, lanes, True)
        + [(dh, dh_out.at[here]), (wa, wa_out.at[here])],
        sems,
        3 * n,
    )
    begin(outs)
    panel = width // PANELS

    def panel_copies(p):
        pairs = row_pairs(dx_out, dx.at[p], counts, step, p * panel, panel, True)
        return copies_of(pairs, out_sems, n * p)

    @pl.loop(0, PANELS)
    def _(p):
        dx[p] = lax.dot_general(
            dh[...], wgu[span(p * panel, panel)], NT, preferred_element_type=F32
        ).astype(BF16)
        begin(panel_copies(p))

    end(outs)
    for p in range(PANELS):
        end(panel_copies(p))


def group_counts(pieces, groups):
    return [p.shape[0] // groups for p in pieces]


def back_rows(me, xds, w_gu, w_dn, groups):
    ff, width = w_dn.shape
    lanes = xds[0].shape[1] - 2 * width
    counts = group_counts(xds, groups)
    rows = sum(counts)
    n = len(counts)
    total = rows * groups
    shape = jax.ShapeDtypeStruct
    out = pl.pallas_call(
        lambda *refs: back_kernel(counts, groups, *refs),
        grid_spec=pltpu.PrefetchScalarGridSpec(
            num_scalar_prefetch=1,
            grid=(groups,),
            in_specs=[ANY] * (n + 2),
            out_specs=[ANY] * (n + 2),
            scratch_shapes=[
                pltpu.VMEM((rows, width), BF16),
                pltpu.VMEM((rows, width), BF16),
                pltpu.VMEM((rows, lanes), BF16),
                pltpu.VMEM(w_gu.shape, BF16),
                pltpu.VMEM(w_dn.shape, BF16),
                pltpu.VMEM((PANELS, rows, width // PANELS), BF16),
                pltpu.VMEM((rows, lanes), BF16),
                pltpu.VMEM((rows, 2 * ff), BF16),
                pltpu.VMEM((rows, ff), BF16),
                pltpu.VMEM((rows, 1), F32),
                pltpu.SemaphoreType.DMA((4 * n + 2,)),
                pltpu.SemaphoreType.DMA((3 * CHUNKS,)),
                pltpu.SemaphoreType.DMA((n * PANELS,)),
            ],
        ),
        out_shape=[shape((p.shape[0], width + lanes), BF16) for p in xds]
        + [shape((total, 2 * ff), BF16), shape((total, ff), BF16)],
        compiler_params=pltpu.CompilerParams(vmem_limit_bytes=VMEM_BYTES),
        cost_estimate=pl.CostEstimate(
            flops=total * width * ff * 10,
            bytes_accessed=6 * ff * width + total * (6 * width + 4 * lanes + 6 * ff),
            transcendentals=total * ff,
        ),
    )(me, *xds, w_gu, w_dn)
    return out[:n], out[n], out[n + 1]


def forward_kernel(counts, groups, me_ref, *refs):
    n = len(counts)
    x_in, (wgu_ref, wdn_ref), y_out = refs[:n], refs[n : n + 2], refs[n + 2 : 2 * n + 2]
    x, table, wgu, wdn, act, y, sems, w_sems, out_sems = refs[2 * n + 2 :]
    step = pl.program_id(0) if groups > 1 else 0
    ff, width = wdn.shape
    lanes = table.shape[1]
    weights = lambda j: weight_copies(wgu_ref, wdn_ref, wgu, wdn, w_sems, j)
    first = once(groups, step)
    ins = copies_of(
        row_pairs(x_in, x, counts, step, 0, width)
        + row_pairs(x_in, table, counts, step, width, lanes),
        sems,
        0,
    )
    begin(ins)

    @first
    def _():
        for j in range(CHUNKS):
            begin(weights(j))

    end(ins)
    wide = ff // CHUNKS

    @pl.loop(0, CHUNKS)
    def _(j):
        first(lambda: end(weights(j)))
        own = span(j * wide, wide)
        also = span(ff + j * wide, wide)
        gate = jnp.dot(x[...], wgu[:, own], preferred_element_type=F32)
        upper = jnp.dot(x[...], wgu[:, also], preferred_element_type=F32)
        act[:, own] = (gate * jax.nn.sigmoid(gate) * upper).astype(BF16)

    panel = width // PANELS

    def panel_copies(p):
        pairs = row_pairs(y_out, y.at[p], counts, step, p * panel, panel, True)
        return copies_of(pairs, out_sems, n * p)

    @pl.loop(0, PANELS)
    def _(p):
        gate_f = pick(table[...], me_ref[1])
        cols = span(p * panel, panel)
        y[p] = (jnp.dot(act[...], wdn[:, cols], preferred_element_type=F32) * gate_f).astype(BF16)
        begin(panel_copies(p))

    for p in range(PANELS):
        end(panel_copies(p))


def forward_rows(me, xs, w_gu, w_dn, groups):
    ff, width = w_dn.shape
    lanes = xs[0].shape[1] - width
    counts = group_counts(xs, groups)
    rows = sum(counts)
    n = len(counts)
    total = rows * groups
    return pl.pallas_call(
        lambda *refs: forward_kernel(counts, groups, *refs),
        grid_spec=pltpu.PrefetchScalarGridSpec(
            num_scalar_prefetch=1,
            grid=(groups,),
            in_specs=[ANY] * (n + 2),
            out_specs=[ANY] * n,
            scratch_shapes=[
                pltpu.VMEM((rows, width), BF16),
                pltpu.VMEM((rows, lanes), BF16),
                pltpu.VMEM(w_gu.shape, BF16),
                pltpu.VMEM(w_dn.shape, BF16),
                pltpu.VMEM((rows, ff), BF16),
                pltpu.VMEM((PANELS, rows, width // PANELS), BF16),
                pltpu.SemaphoreType.DMA((2 * n,)),
                pltpu.SemaphoreType.DMA((3 * CHUNKS,)),
                pltpu.SemaphoreType.DMA((n * PANELS,)),
            ],
        ),
        out_shape=[jax.ShapeDtypeStruct((p.shape[0], width), BF16) for p in xs],
        compiler_params=pltpu.CompilerParams(vmem_limit_bytes=VMEM_BYTES),
        cost_estimate=pl.CostEstimate(
            flops=total * width * ff * 6,
            bytes_accessed=6 * ff * width + total * 4 * width,
            transcendentals=total * ff,
        ),
    )(me, *xs, w_gu, w_dn)


def weight_kernel(lefts, rights, left_at, right_at, groups, *refs):
    n, m = len(lefts), len(rights)
    left_in, right_in, out_ref = refs[:n], refs[n : n + m], refs[n + m]
    left, right, stage = refs[n + m + 1 : n + m + 4]
    sems, left_sems, out_sems = refs[-3:]
    step = pl.program_id(0) if groups > 1 else 0
    tiles, _, tile = left.shape
    rights_made = copies_of(row_pairs(right_in, right, rights, step, right_at, right.shape[1]), sems, 0)
    begin(rights_made)

    def left_copies(t):
        pairs = row_pairs(left_in, left.at[t], lefts, step, left_at + t * tile, tile)
        return copies_of(pairs, left_sems, n * t)

    def out_copy(t):
        return copies_of([(stage.at[t], out_ref.at[span(t * tile, tile)])], out_sems, t)

    for t in range(tiles):
        begin(left_copies(t))
    end(rights_made)

    @pl.loop(0, tiles)
    def _(t):
        end(left_copies(t))
        part = lax.dot_general(left[t], right[...], TN, preferred_element_type=F32)
        if groups > 1:
            total = refs[n + m + 4]
            part += jnp.where(step == 0, 0.0, total[t])
            total[t] = part
            stage[t] = part.astype(BF16)
            pl.when(step == groups - 1)(lambda: begin(out_copy(t)))
        else:
            stage[t] = part.astype(BF16)
            begin(out_copy(t))

    def finish():
        for t in range(tiles):
            end(out_copy(t))

    pl.when(step == groups - 1)(finish) if groups > 1 else finish()


def weight_grad(lefts, rights, left_at, left_wide, right_at, right_wide, groups):
    left_counts = group_counts(lefts, groups)
    right_counts = group_counts(rights, groups)
    rows = sum(left_counts)
    tile = 256
    tiles = left_wide // tile
    scratch = [
        pltpu.VMEM((tiles, rows, tile), BF16),
        pltpu.VMEM((rows, right_wide), BF16),
        pltpu.VMEM((tiles, tile, right_wide), BF16),
    ]
    if groups > 1:
        scratch.append(pltpu.VMEM((tiles, tile, right_wide), F32))
    scratch += [pltpu.SemaphoreType.DMA((k,)) for k in (len(rights), tiles * len(lefts), tiles)]
    return pl.pallas_call(
        lambda *refs: weight_kernel(left_counts, right_counts, left_at, right_at, groups, *refs),
        grid=(groups,),
        in_specs=[ANY] * (len(lefts) + len(rights)),
        out_specs=ANY,
        out_shape=jax.ShapeDtypeStruct((left_wide, right_wide), BF16),
        scratch_shapes=scratch,
        compiler_params=pltpu.CompilerParams(vmem_limit_bytes=VMEM_BYTES),
        cost_estimate=pl.CostEstimate(
            flops=2 * rows * groups * left_wide * right_wide,
            bytes_accessed=2 * rows * groups * (left_wide + right_wide) + 2 * left_wide * right_wide,
            transcendentals=0,
        ),
    )(*lefts, *rights)


def shards(
    fwd_tokens,
    fwd_routes,
    fwd_gates,
    bwd_tokens,
    bwd_routes,
    bwd_gates,
    cotangent,
    w_gate_up,
    w_down,
):
    size = lax.axis_size("expert")
    me = lax.axis_index("expert")
    count, width = fwd_tokens.shape[1:]
    w_gu = w_gate_up[0, 0]
    w_dn = w_down[0, 0]
    ff = w_dn.shape[0]
    groups = max(1, size // 16)
    sections = lax.axis_size("segment")
    swap = [(s, s ^ 1) for s in range(sections)]
    table = jnp.concatenate(
        [
            dense_gates(bwd_routes[0], bwd_gates[0], size),
            dense_gates(fwd_routes[0], fwd_gates[0], size),
        ],
        axis=1,
    )
    table = jnp.pad(table, ((0, 0), (0, -table.shape[1] % LANES))).astype(BF16)
    places = jnp.stack([me, me + size]).astype(jnp.int32)
    parts = three_ways(size, count)
    first = send(fwd_tokens[0], size, top_bit(size))
    tables = table, send(table, size, top_bit(size))
    pair = [jnp.concatenate(both, axis=1) for both in zip((fwd_tokens[0], first), tables)]
    pair = [jnp.concatenate([p[a:b] for p in pair]) for a, b, _ in parts]
    xf_kept, xf_new = spread_rest(pair, size, parts)
    y_kept = forward_rows(places, xf_kept, w_gu, w_dn, groups)

    def forward_new(xf_new):
        return forward_rows(places, xf_new, w_gu, w_dn, groups)

    def forward_first(y_kept, y_new, *hold):
        return collect_first(y_kept, y_new, size, parts, hold)

    def forward_last(rows):
        return collect_rest(rows, size, parts).astype(BF16)

    xd_in = jnp.concatenate([bwd_tokens[0], cotangent[0], table], axis=1)
    if groups > 1:
        y_new = forward_new(after(xf_new, y_kept))
        combined = forward_last(forward_first(y_kept, y_new))
        xd_in = after(xd_in, combined)
    xd_in = after(xd_in, first)
    pair = xd_in, send(xd_in, size, top_bit(size))
    pair = [jnp.concatenate([p[a:b] for p in pair]) for a, b, _ in parts]
    xd_kept, xd_new = spread_rest(pair, size, parts)
    other_routes = lax.ppermute(bwd_routes[0], "segment", swap)

    if groups == 1:
        y_new = forward_new(after(xf_new, y_kept))
        xd_kept = after(xd_kept, y_new)
    dx_kept, dh_kept, wa_kept = back_rows(places, xd_kept, w_gu, w_dn, groups)
    xd_new = after(xd_new, dx_kept)
    if groups == 1:
        y_new = after(y_new, xd_new)
    dx_new, dh_new, wa_new = back_rows(places, xd_new, w_gu, w_dn, groups)
    if groups == 1:
        comb_rows = forward_first(y_kept, y_new, dx_new)
        wa_kept = after(wa_kept, comb_rows)
    home_rows = collect_first(dx_kept, dx_new, size, parts, ())
    if groups == 1:
        combined = forward_last(comb_rows)
    home = collect_rest(home_rows, size, parts)

    xds = [*xd_kept, *xd_new]
    grad_gu = weight_grad(xds, [dh_kept, dh_new], 0, width, 0, 2 * ff, groups)
    grad_dn = weight_grad([wa_kept, wa_new], xds, 0, ff, width, width, groups)

    token_grad = home[:, :width].astype(BF16)
    hit = other_routes[:, :, None] == jnp.arange(size, dtype=jnp.int32)[None, None, :]
    gate_home = jnp.sum(jnp.where(hit, home[:, None, width : width + size], 0.0), axis=2)
    return (
        combined[None],
        token_grad[None],
        gate_home.astype(BF16)[None],
        grad_gu[None, None],
        grad_dn[None, None],
    )


def solution(mesh):
    three = P("segment", "expert", None)
    four = P("segment", "expert", None, None)

    return jax.shard_map(
        shards,
        mesh=mesh,
        in_specs=(three,) * 7 + (four,) * 2,
        out_specs=(three,) * 3 + (four,) * 2,
        check_vma=False,
    )
```

profile of v0, /device:TPU:13, one launch (start us, length us, event | category | flops | bytes accessed | tf_op | source)
XLA Modules:
  0.0 256.4 jit_solution(695279582447256045)
XLA Ops:
  0.6 0.7 bitcast_convert_fusion
  1.4 0.7 bitcast_convert_fusion.1
  2.1 0.7 select_reduce_fusion.2
  2.9 0.7 select_reduce_fusion.1
  3.8 2.3 collective-permute-start.1
  6.1 1.0 pad_maximum_fusion.23
  7.2 1.1 pad_maximum_fusion.8
  8.3 10.1 %collective-permute-done = bf16[64,2048]{1,0:T(8,128)(2,1)S(1)} collective-permute-done((bf16[64,2048]{1,0:T(8,128)(2,1)}, bf16[64,2048]{1,0:T(8,128)(2,1)S(1)}, u32[]{:S(2)}, u32[]{:S(2)}) %collective-permute-start) | collective-permute-done | bytes 262176 | tf_op jit(solution)/shard_map/ppermute | solution.py:23
  18.5 3.1 %collective-permute-start.11 = (bf16[64,4224]{1,0:T(8,128)(2,1)S(1)}, bf16[64,4224]{1,0:T(8,128)(2,1)S(1)}, u32[]{:S(2)}, u32[]{:S(2)}) collective-permute-start(bf16[64,4224]{1,0:T(8,128)(2,1)S(1)} %pad_maximum_fusion.8), channel_id=1, source_target_pairs={{0,8},{1,9},{2,10},{3,11},{4,12},{5,13},{6,14},{7,15},{8,0},{9,1},... | collective-permute-start | bytes 1622024 | tf_op jit(solution)/shard_map/ppermute | solution.py:23
  21.6 1.3 collective-permute-start.2
  23.3 2.8 %collective-permute-done.2 = bf16[32,2176]{1,0:T(8,128)(2,1)S(1)} collective-permute-done((bf16[32,2176]{1,0:T(8,128)(2,1)S(1)}, bf16[32,2176]{1,0:T(8,128)(2,1)S(1)}, u32[]{:S(2)}, u32[]{:S(2)}) %collective-permute-start.2) | collective-permute-done | bytes 139296 | tf_op jit(solution)/shard_map/ppermute | solution.py:23
  26.4 2.2 collective-permute-done.4
  28.7 7.3 %collective-permute-done.6 = bf16[48,2176]{1,0:T(8,128)(2,1)S(1)} collective-permute-done((bf16[48,2176]{1,0:T(8,128)(2,1)S(1)}, bf16[48,2176]{1,0:T(8,128)(2,1)S(1)}, u32[]{:S(2)}, u32[]{:S(2)}) %collective-permute-start.6) | collective-permute-done | bytes 208928 | tf_op jit(solution)/shard_map/ppermute | solution.py:23
  36.1 1.3 collective-permute-start.7
  37.5 6.2 %collective-permute-done.11 = bf16[64,4224]{1,0:T(8,128)(2,1)S(1)} collective-permute-done((bf16[64,4224]{1,0:T(8,128)(2,1)S(1)}, bf16[64,4224]{1,0:T(8,128)(2,1)S(1)}, u32[]{:S(2)}, u32[]{:S(2)}) %collective-permute-start.11) | collective-permute-done | bytes 540704 | tf_op jit(solution)/shard_map/ppermute | solution.py:23
  43.8 1.3 collective-permute-start.12
  45.5 3.4 %collective-permute-start.18 = (bf16[48,4224]{1,0:T(8,128)(2,1)S(1)}, bf16[48,4224]{1,0:T(8,128)(2,1)S(1)}, u32[]{:S(2)}, u32[]{:S(2)}) collective-permute-start(bf16[48,4224]{1,0:T(8,128)(2,1)S(1)} %pad_maximum_fusion.13), channel_id=1, source_target_pairs={{0,4},{1,5},{2,6},{3,7},{4,0},{5,1},{6,2},{7,3},{8,12},{9,13},{10,... | collective-permute-start | bytes 1216520 | tf_op jit(solution)/shard_map/ppermute | solution.py:23
  49.0 1.3 collective-permute-start.10
  50.3 10.9 %shard_map.128 = (bf16[128,2048]{1,0:T(8,128)(2,1)S(1)}, bf16[192,2048]{1,0:T(8,128)(2,1)S(1)}, bf16[192,2048]{1,0:T(8,128)(2,1)S(1)}) custom-call(s32[2]{0:T(128)S(1)} %pad_add_fusion.refs_0_, bf16[128,2176]{1,0:T(8,128)(2,1)S(1)} %pad_maximum_fusion.7.refs_1_, bf16[192,2176]{1,0:T(8,128)(2,1)S(1)} %pad_maximum_fusion.3.refs_2_, ...), custom_call_target="tpu_custom_call" | custom-call | flops 4831838208 | bytes 13631488 | tf_op jit(solution)/shard_map/pallas_call | solution.py:335
  61.2 5.7 %collective-permute-done.18 = bf16[48,4224]{1,0:T(8,128)(2,1)S(1)} collective-permute-done((bf16[48,4224]{1,0:T(8,128)(2,1)S(1)}, bf16[48,4224]{1,0:T(8,128)(2,1)S(1)}, u32[]{:S(2)}, u32[]{:S(2)}) %collective-permute-start.18) | collective-permute-done | bytes 405536 | tf_op jit(solution)/shard_map/ppermute | solution.py:23
  66.9 1.2 collective-permute-start.9
  68.6 2.3 collective-permute-start.16
  71.0 29.8 %collective-permute-done.19 = bf16[96,4224]{1,0:T(8,128)(2,1)S(1)} collective-permute-done((bf16[96,4224]{1,0:T(8,128)(2,1)S(1)}, bf16[96,4224]{1,0:T(8,128)(2,1)S(1)}, u32[]{:S(2)}, u32[]{:S(2)}) %collective-permute-start.19) | collective-permute-done | bytes 811040 | tf_op jit(solution)/shard_map/ppermute | solution.py:23
  100.7 0.4 collective-permute-start.13
  101.3 1.2 collective-permute-start.20
  102.4 1.3 pad_maximum_fusion.refs_2_.refs_1_.refs_3_
  103.8 6.2 %collective-permute-done.13 = bf16[64,4224]{1,0:T(8,128)(2,1)S(1)} collective-permute-done((bf16[64,4224]{1,0:T(8,128)(2,1)S(1)}, bf16[64,4224]{1,0:T(8,128)(2,1)S(1)}, u32[]{:S(2)}, u32[]{:S(2)}) %collective-permute-start.13) | collective-permute-done | bytes 540704 | tf_op jit(solution)/shard_map/ppermute | solution.py:23
  110.0 3.1 %collective-permute-start.17 = (bf16[192,4224]{1,0:T(8,128)(2,1)}, bf16[192,4224]{1,0:T(8,128)(2,1)}, u32[]{:S(2)}, u32[]{:S(2)}) collective-permute-start(bf16[192,4224]{1,0:T(8,128)(2,1)} %pad_maximum_fusion.refs_2_.refs_1_.refs_3_), channel_id=1, source_target_pairs={{0,1},{1,0},{2,3},{3,2},{4,5},{5,4},{6,7},{7,6},{8,9},{9,8},{10,11... | collective-permute-start | bytes 4866056 | tf_op jit(solution)/shard_map/ppermute | solution.py:23
  113.2 8.9 %collective-permute-start.43 = (s32[64,8]{0,1:T(8,128)S(1)}, s32[64,8]{0,1:T(8,128)S(1)}, u32[]{:S(2)}, u32[]{:S(2)}) collective-permute-start(s32[64,8]{0,1:T(8,128)S(1)} %bitcast.32), channel_id=1, source_target_pairs={{0,16},{16,0},{1,17},{17,1},{2,18},{18,2},{3,19},{19,3},{4,20},{20... | collective-permute-start | bytes 6152 | tf_op jit(solution)/shard_map/ppermute | solution.py:491
  122.2 2.2 collective-permute-start.14
  124.4 10.9 %shard_map.129 = (bf16[128,2048]{1,0:T(8,128)(2,1)S(1)}, bf16[192,2048]{1,0:T(8,128)(2,1)S(1)}, bf16[192,2048]{1,0:T(8,128)(2,1)S(1)}) custom-call(s32[2]{0:T(128)S(1)} %pad_add_fusion.refs_0_, bf16[128,2176]{1,0:T(8,128)(2,1)S(1)} %collective-permute-done.8.refs_1_, bf16[192,2176]{1,0:T(8,128)(2,1)S(1)} %collective-permute-done.9.refs_2_, ...), custom_call_target="tpu_custom_call" | custom-call | flops 4831838208 | bytes 13631488 | tf_op jit(solution)/shard_map/pallas_call | solution.py:335
  135.2 15.5 %shard_map.130 = (bf16[128,2176]{1,0:T(8,128)(2,1)S(1)}, bf16[192,2176]{1,0:T(8,128)(2,1)S(1)}, bf16[192,2176]{1,0:T(8,128)(2,1)S(1)}, bf16[512,1536]{1,0:T(8,128)(2,1)}, bf16[512,768]{1,0:T(8,128)(2,1)S(1)}) custom-call(s32[2]{0:T(128)S(1)} %pad_add_fusion.refs_0_, bf16[128,4224]{1,0:T(8,128)(2,1)S(1)} %pad_maximum_fusion.2.refs_1_.refs_0_.refs_2_, ...), custom_call_target="tpu_custom_call" | custom-call | flops 8053063680 | bytes 18350080 | tf_op jit(solution)/shard_map/pallas_call | solution.py:242
  151.5 15.5 %shard_map.131 = (bf16[128,2176]{1,0:T(8,128)(2,1)S(1)}, bf16[192,2176]{1,0:T(8,128)(2,1)S(1)}, bf16[192,2176]{1,0:T(8,128)(2,1)S(1)}, bf16[512,1536]{1,0:T(8,128)(2,1)}, bf16[512,768]{1,0:T(8,128)(2,1)S(1)}) custom-call(s32[2]{0:T(128)S(1)} %pad_add_fusion.refs_0_, bf16[128,4224]{1,0:T(8,128)(2,1)S(1)} %collective-permute-done.14.refs_1_.refs_3_.refs_5_, ...), custom_call_target="tpu_custom_call" | custom-call | flops 8053063680 | bytes 18350080 | tf_op jit(solution)/shard_map/pallas_call | solution.py:242
  167.0 0.9 collective-permute-start.21
  168.0 0.6 collective-permute-start.32
  168.6 11.1 %shard_map.132 = bf16[2048,1536]{1,0:T(8,128)(2,1)} custom-call(bf16[128,4224]{1,0:T(8,128)(2,1)S(1)} %pad_maximum_fusion.2.refs_1_.refs_0_.refs_2_, bf16[192,4224]{1,0:T(8,128)(2,1)} %pad_maximum_fusion.refs_2_.refs_1_.refs_3_, bf16[192,4224]{1,0:T(8,128)(2,1)} %copy-done.1, bf16[128,4224]{1,0:T(8,128)(2,1)S(1)} %collective-permute-done.14.refs_1_.refs_3_.refs_5_, ...), custom_call_target="tpu_custom_call" | custom-call | flops 6442450944 | bytes 13631488 | tf_op jit(solution)/shard_map/pallas_call | solution.py:420
  179.7 0.8 copy-done.4
  180.4 1.2 collective-permute-start.33
  181.6 1.2 collective-permute-start.34
  182.8 1.4 add_convert_fusion.7
  184.3 0.4 collective-permute-start.24
  184.7 1.4 add_convert_fusion.5
  186.1 6.9 %shard_map.133 = bf16[768,2048]{1,0:T(8,128)(2,1)} custom-call(bf16[512,768]{1,0:T(8,128)(2,1)S(1)} %get-tuple-element.75.refs_0_, bf16[512,768]{1,0:T(8,128)(2,1)S(1)} %get-tuple-element.76.refs_1_, bf16[128,4224]{1,0:T(8,128)(2,1)S(1)} %pad_maximum_fusion.2.refs_1_.refs_0_.refs_2_, bf16[192,4224]{1,0:T(8,128)(2,1)} %pad_maximum_fusion.refs_2_.refs_1_.refs_3_, ...), custom_call_target="tpu_custom_call" | custom-call | flops 3221225472 | bytes 8912896 | tf_op jit(solution)/shard_map/pallas_call | solution.py:420
  193.3 3.1 %collective-permute-done.33 = bf16[192,2176]{1,0:T(8,128)(2,1)S(1)} collective-permute-done((bf16[192,2176]{1,0:T(8,128)(2,1)S(1)}, bf16[192,2176]{1,0:T(8,128)(2,1)S(1)}, u32[]{:S(2)}, u32[]{:S(2)}) %collective-permute-start.33) | collective-permute-done | bytes 835616 | tf_op jit(solution)/shard_map/ppermute | solution.py:23
  196.4 1.9 collective-permute-done.34
  198.7 1.2 add_convert_fusion.9
  199.9 1.3 collective-permute-start.35
  201.2 2.8 %collective-permute-done.24 = bf16[64,2048]{1,0:T(8,128)(2,1)S(1)} collective-permute-done((bf16[64,2048]{1,0:T(8,128)(2,1)S(1)}, bf16[64,2048]{1,0:T(8,128)(2,1)S(1)}, u32[]{:S(2)}, u32[]{:S(2)}) %collective-permute-start.24) | collective-permute-done | bytes 262176 | tf_op jit(solution)/shard_map/ppermute | solution.py:23
  204.0 5.9 %collective-permute-done.35 = bf16[64,2176]{1,0:T(8,128)(2,1)S(1)} collective-permute-done((bf16[64,2176]{1,0:T(8,128)(2,1)S(1)}, bf16[64,2176]{1,0:T(8,128)(2,1)S(1)}, u32[]{:S(2)}, u32[]{:S(2)}) %collective-permute-start.35) | collective-permute-done | bytes 278560 | tf_op jit(solution)/shard_map/ppermute | solution.py:23
  210.0 0.5 collective-permute-start.25
  210.7 1.1 collective-permute-start.36
  211.8 4.5 %collective-permute-done.25 = bf16[32,2048]{1,0:T(8,128)(2,1)S(1)} collective-permute-done((bf16[32,2048]{1,0:T(8,128)(2,1)S(1)}, bf16[32,2048]{1,0:T(8,128)(2,1)S(1)}, u32[]{:S(2)}, u32[]{:S(2)}) %collective-permute-start.25) | collective-permute-done | bytes 131104 | tf_op jit(solution)/shard_map/ppermute | solution.py:23
  216.3 0.9 collective-permute-start.29
  217.2 1.2 collective-permute-start.27
  218.5 0.7 collective-permute-start.40
  219.3 1.1 collective-permute-start.38
  220.5 2.7 %collective-permute-done.29 = bf16[48,2048]{1,0:T(8,128)(2,1)S(1)} collective-permute-done((bf16[48,2048]{1,0:T(8,128)(2,1)S(1)}, bf16[48,2048]{1,0:T(8,128)(2,1)S(1)}, u32[]{:S(2)}, u32[]{:S(2)}) %collective-permute-start.29) | collective-permute-done | bytes 196640 | tf_op jit(solution)/shard_map/ppermute | solution.py:23
  223.4 8.6 %collective-permute-start.31 = (bf16[64,2048]{1,0:T(8,128)(2,1)S(1)}, bf16[64,2048]{1,0:T(8,128)(2,1)S(1)}, u32[]{:S(2)}, u32[]{:S(2)}) collective-permute-start(bf16[64,2048]{1,0:T(8,128)(2,1)S(1)} %pad_maximum_fusion.19), channel_id=1, source_target_pairs={{0,24},{1,25},{2,26},{3,27},{4,28},{5,29},{6,30},{7,31},{8,16},{9,... | collective-permute-start | bytes 786440 | tf_op jit(solution)/shard_map/ppermute | solution.py:84
  232.3 3.9 %collective-permute-start.42 = (bf16[64,2176]{1,0:T(8,128)(2,1)S(1)}, bf16[64,2176]{1,0:T(8,128)(2,1)S(1)}, u32[]{:S(2)}, u32[]{:S(2)}) collective-permute-start(bf16[64,2176]{1,0:T(8,128)(2,1)S(1)} %pad_maximum_fusion.16), channel_id=1, source_target_pairs={{0,24},{1,25},{2,26},{3,27},{4,28},{5,29},{6,30},{7,31},{8,16},{9,... | collective-permute-start | bytes 835592 | tf_op jit(solution)/shard_map/ppermute | solution.py:84
  236.3 12.7 %collective-permute-done.31 = bf16[64,2048]{1,0:T(8,128)(2,1)S(1)} collective-permute-done((bf16[64,2048]{1,0:T(8,128)(2,1)S(1)}, bf16[64,2048]{1,0:T(8,128)(2,1)S(1)}, u32[]{:S(2)}, u32[]{:S(2)}) %collective-permute-start.31) | collective-permute-done | bytes 262176 | tf_op jit(solution)/shard_map/ppermute | solution.py:84
  248.9 0.8 fusion
  249.7 5.2 %collective-permute-done.42 = bf16[64,2176]{1,0:T(8,128)(2,1)S(1)} collective-permute-done((bf16[64,2176]{1,0:T(8,128)(2,1)S(1)}, bf16[64,2176]{1,0:T(8,128)(2,1)S(1)}, u32[]{:S(2)}, u32[]{:S(2)}) %collective-permute-start.42) | collective-permute-done | bytes 278560 | tf_op jit(solution)/shard_map/ppermute | solution.py:84
  255.0 0.7 fusion.1
  255.8 0.6 select_reduce_fusion
  (111 shorter events, 5.6 us)
Async XLA Ops:
  0.6 7.7 %copy-start.2 = (bf16[1,64,2048]{2,1,0:T(8,128)(2,1)S(1)}, bf16[1,64,2048]{2,1,0:T(8,128)(2,1)}, u32[]{:S(2)}) copy-start(bf16[1,64,2048]{2,1,0:T(8,128)(2,1)} %param.9) | copy-start | bytes 786436
  3.8 14.7 %collective-permute-start.1 = (bf16[64,128]{1,0:T(8,128)(2,1)S(1)}, bf16[64,128]{1,0:T(8,128)(2,1)S(1)}, u32[]{:S(2)}, u32[]{:S(2)}) collective-permute-start(bf16[64,128]{1,0:T(8,128)(2,1)S(1)} %fusion.4), channel_id=1, source_target_pairs={{0,8},{1,9},{2,10},{3,11},{4,12},{5,13},{6,14},{7,15},{8,0},{9,1},... | collective-permute-start | bytes 49160 | tf_op jit(solution)/shard_map/ppermute | solution.py:23
  6.1 12.3 %collective-permute-start = (bf16[64,2048]{1,0:T(8,128)(2,1)}, bf16[64,2048]{1,0:T(8,128)(2,1)S(1)}, u32[]{:S(2)}, u32[]{:S(2)}) collective-permute-start(bf16[64,2048]{1,0:T(8,128)(2,1)} %bitcast.25), channel_id=1, source_target_pairs={{0,8},{1,9},{2,10},{3,11},{4,12},{5,13},{6,14},{7,15},{8,0},{9,1},... | collective-permute-start | bytes 786440 | tf_op jit(solution)/shard_map/ppermute | solution.py:23
  18.5 25.2 %collective-permute-start.11 = (bf16[64,4224]{1,0:T(8,128)(2,1)S(1)}, bf16[64,4224]{1,0:T(8,128)(2,1)S(1)}, u32[]{:S(2)}, u32[]{:S(2)}) collective-permute-start(bf16[64,4224]{1,0:T(8,128)(2,1)S(1)} %pad_maximum_fusion.8), channel_id=1, source_target_pairs={{0,8},{1,9},{2,10},{3,11},{4,12},{5,13},{6,14},{7,15},{8,0},{9,1},... | collective-permute-start | bytes 1622024 | tf_op jit(solution)/shard_map/ppermute | solution.py:23
  21.6 4.5 %collective-permute-start.2 = (bf16[32,2176]{1,0:T(8,128)(2,1)S(1)}, bf16[32,2176]{1,0:T(8,128)(2,1)S(1)}, u32[]{:S(2)}, u32[]{:S(2)}) collective-permute-start(bf16[32,2176]{1,0:T(8,128)(2,1)S(1)} %pad_maximum_fusion.22), channel_id=1, source_target_pairs={{0,1},{1,0},{2,3},{3,2},{4,5},{5,4},{6,7},{7,6},{8,9},{9,8},{10,11... | collective-permute-start | bytes 417800 | tf_op jit(solution)/shard_map/ppermute | solution.py:23
  22.9 5.7 %collective-permute-start.4 = (bf16[48,2176]{1,0:T(8,128)(2,1)S(1)}, bf16[48,2176]{1,0:T(8,128)(2,1)S(1)}, u32[]{:S(2)}, u32[]{:S(2)}) collective-permute-start(bf16[48,2176]{1,0:T(8,128)(2,1)S(1)} %pad_maximum_fusion.20), channel_id=1, source_target_pairs={{0,2},{1,3},{2,0},{3,1},{4,6},{5,7},{6,4},{7,5},{8,10},{9,11},{10,... | collective-permute-start | bytes 626696 | tf_op jit(solution)/shard_map/ppermute | solution.py:23
  23.2 12.8 %collective-permute-start.6 = (bf16[48,2176]{1,0:T(8,128)(2,1)S(1)}, bf16[48,2176]{1,0:T(8,128)(2,1)S(1)}, u32[]{:S(2)}, u32[]{:S(2)}) collective-permute-start(bf16[48,2176]{1,0:T(8,128)(2,1)S(1)} %pad_maximum_fusion.21), channel_id=1, source_target_pairs={{0,4},{1,5},{2,6},{3,7},{4,0},{5,1},{6,2},{7,3},{8,12},{9,13},{10,... | collective-permute-start | bytes 626696 | tf_op jit(solution)/shard_map/ppermute | solution.py:23
  26.1 11.2 %collective-permute-start.3 = (bf16[64,2176]{1,0:T(8,128)(2,1)S(1)}, bf16[64,2176]{1,0:T(8,128)(2,1)S(1)}, u32[]{:S(2)}, u32[]{:S(2)}) collective-permute-start(bf16[64,2176]{1,0:T(8,128)(2,1)S(1)} %pad_maximum_fusion.14), channel_id=1, source_target_pairs={{0,2},{1,3},{2,0},{3,1},{4,6},{5,7},{6,4},{7,5},{8,10},{9,11},{10,... | collective-permute-start | bytes 835592 | tf_op jit(solution)/shard_map/ppermute | solution.py:23
  28.7 20.3 %collective-permute-start.5 = (bf16[96,2176]{1,0:T(8,128)(2,1)S(1)}, bf16[96,2176]{1,0:T(8,128)(2,1)S(1)}, u32[]{:S(2)}, u32[]{:S(2)}) collective-permute-start(bf16[96,2176]{1,0:T(8,128)(2,1)S(1)} %pad_maximum_fusion.10), channel_id=1, source_target_pairs={{0,4},{1,5},{2,6},{3,7},{4,0},{5,1},{6,2},{7,3},{8,12},{9,13},{10,... | collective-permute-start | bytes 1253384 | tf_op jit(solution)/shard_map/ppermute | solution.py:23
  36.1 9.4 %collective-permute-start.7 = (bf16[96,2176]{1,0:T(8,128)(2,1)S(1)}, bf16[96,2176]{1,0:T(8,128)(2,1)S(1)}, u32[]{:S(2)}, u32[]{:S(2)}) collective-permute-start(bf16[96,2176]{1,0:T(8,128)(2,1)S(1)} %pad_maximum_fusion.11), channel_id=1, source_target_pairs={{0,1},{1,0},{2,3},{3,2},{4,5},{5,4},{6,7},{7,6},{8,9},{9,8},{10,11... | collective-permute-start | bytes 1253384 | tf_op jit(solution)/shard_map/ppermute | solution.py:23
  37.4 75.8 %collective-permute-start.8 = (bf16[128,2176]{1,0:T(8,128)(2,1)S(1)}, bf16[128,2176]{1,0:T(8,128)(2,1)S(1)}, u32[]{:S(2)}, u32[]{:S(2)}) collective-permute-start(bf16[128,2176]{1,0:T(8,128)(2,1)S(1)} %pad_maximum_fusion.7.refs_1_), channel_id=1, source_target_pairs={{0,4},{1,5},{2,6},{3,7},{4,0},{5,1},{6,2},{7,3},{8,12},{9,13},{10,... | collective-permute-start | bytes 1671176 | tf_op jit(solution)/shard_map/ppermute | solution.py:23
  43.8 24.8 %collective-permute-start.12 = (bf16[32,4224]{1,0:T(8,128)(2,1)S(1)}, bf16[32,4224]{1,0:T(8,128)(2,1)S(1)}, u32[]{:S(2)}, u32[]{:S(2)}) collective-permute-start(bf16[32,4224]{1,0:T(8,128)(2,1)S(1)} %pad_maximum_fusion.17), channel_id=1, source_target_pairs={{0,1},{1,0},{2,3},{3,2},{4,5},{5,4},{6,7},{7,6},{8,9},{9,8},{10,11... | collective-permute-start | bytes 811016 | tf_op jit(solution)/shard_map/ppermute | solution.py:23
  45.1 23.1 %collective-permute-start.15 = (bf16[48,4224]{1,0:T(8,128)(2,1)S(1)}, bf16[48,4224]{1,0:T(8,128)(2,1)S(1)}, u32[]{:S(2)}, u32[]{:S(2)}) collective-permute-start(bf16[48,4224]{1,0:T(8,128)(2,1)S(1)} %pad_maximum_fusion.12), channel_id=1, source_target_pairs={{0,2},{1,3},{2,0},{3,1},{4,6},{5,7},{6,4},{7,5},{8,10},{9,11},{10,... | collective-permute-start | bytes 1216520 | tf_op jit(solution)/shard_map/ppermute | solution.py:23
  45.5 21.5 %collective-permute-start.18 = (bf16[48,4224]{1,0:T(8,128)(2,1)S(1)}, bf16[48,4224]{1,0:T(8,128)(2,1)S(1)}, u32[]{:S(2)}, u32[]{:S(2)}) collective-permute-start(bf16[48,4224]{1,0:T(8,128)(2,1)S(1)} %pad_maximum_fusion.13), channel_id=1, source_target_pairs={{0,4},{1,5},{2,6},{3,7},{4,0},{5,1},{6,2},{7,3},{8,12},{9,13},{10,... | collective-permute-start | bytes 1216520 | tf_op jit(solution)/shard_map/ppermute | solution.py:23
  48.9 1.4 copy-start.3
  49.0 73.2 %collective-permute-start.10 = (bf16[192,2176]{1,0:T(8,128)(2,1)S(1)}, bf16[192,2176]{1,0:T(8,128)(2,1)S(1)}, u32[]{:S(2)}, u32[]{:S(2)}) collective-permute-start(bf16[192,2176]{1,0:T(8,128)(2,1)S(1)} %pad_maximum_fusion.4.refs_3_), channel_id=1, source_target_pairs={{0,2},{1,3},{2,0},{3,1},{4,6},{5,7},{6,4},{7,5},{8,10},{9,11},{10,... | collective-permute-start | bytes 2506760 | tf_op jit(solution)/shard_map/ppermute | solution.py:23
  66.9 57.4 %collective-permute-start.9 = (bf16[192,2176]{1,0:T(8,128)(2,1)S(1)}, bf16[192,2176]{1,0:T(8,128)(2,1)S(1)}, u32[]{:S(2)}, u32[]{:S(2)}) collective-permute-start(bf16[192,2176]{1,0:T(8,128)(2,1)S(1)} %pad_maximum_fusion.3.refs_2_), channel_id=1, source_target_pairs={{0,1},{1,0},{2,3},{3,2},{4,5},{5,4},{6,7},{7,6},{8,9},{9,8},{10,11... | collective-permute-start | bytes 2506760 | tf_op jit(solution)/shard_map/ppermute | solution.py:23
  68.2 32.5 %collective-permute-start.19 = (bf16[96,4224]{1,0:T(8,128)(2,1)S(1)}, bf16[96,4224]{1,0:T(8,128)(2,1)S(1)}, u32[]{:S(2)}, u32[]{:S(2)}) collective-permute-start(bf16[96,4224]{1,0:T(8,128)(2,1)S(1)} %pad_maximum_fusion.6), channel_id=1, source_target_pairs={{0,1},{1,0},{2,3},{3,2},{4,5},{5,4},{6,7},{7,6},{8,9},{9,8},{10,11... | collective-permute-start | bytes 2433032 | tf_op jit(solution)/shard_map/ppermute | solution.py:23
  68.6 32.6 %collective-permute-start.16 = (bf16[96,4224]{1,0:T(8,128)(2,1)S(1)}, bf16[96,4224]{1,0:T(8,128)(2,1)S(1)}, u32[]{:S(2)}, u32[]{:S(2)}) collective-permute-start(bf16[96,4224]{1,0:T(8,128)(2,1)S(1)} %pad_maximum_fusion.5), channel_id=1, source_target_pairs={{0,4},{1,5},{2,6},{3,7},{4,0},{5,1},{6,2},{7,3},{8,12},{9,13},{10,... | collective-permute-start | bytes 2433032 | tf_op jit(solution)/shard_map/ppermute | solution.py:23
  100.7 9.2 %collective-permute-start.13 = (bf16[64,4224]{1,0:T(8,128)(2,1)S(1)}, bf16[64,4224]{1,0:T(8,128)(2,1)S(1)}, u32[]{:S(2)}, u32[]{:S(2)}) collective-permute-start(bf16[64,4224]{1,0:T(8,128)(2,1)S(1)} %pad_maximum_fusion.9), channel_id=1, source_target_pairs={{0,2},{1,3},{2,0},{3,1},{4,6},{5,7},{6,4},{7,5},{8,10},{9,11},{10,... | collective-permute-start | bytes 1622024 | tf_op jit(solution)/shard_map/ppermute | solution.py:23
  101.2 11.9 %copy-start.1 = (bf16[192,4224]{1,0:T(8,128)(2,1)}, bf16[192,4224]{1,0:T(8,128)(2,1)S(1)}, u32[]{:S(2)}) copy-start(bf16[192,4224]{1,0:T(8,128)(2,1)S(1)} %pad_maximum_fusion.1.refs_3_.refs_2_.refs_4_) | copy-start | bytes 4866052
  101.3 49.5 %collective-permute-start.20 = (bf16[192,4224]{1,0:T(8,128)(2,1)S(1)}, bf16[192,4224]{1,0:T(8,128)(2,1)}, u32[]{:S(2)}, u32[]{:S(2)}) collective-permute-start(bf16[192,4224]{1,0:T(8,128)(2,1)S(1)} %pad_maximum_fusion.1.refs_3_.refs_2_.refs_4_), channel_id=1, source_target_pairs={{0,2},{1,3},{2,0},{3,1},{4,6},{5,7},{6,4},{7,5},{8,10},{9,11},{10,... | collective-permute-start | bytes 4866056 | tf_op jit(solution)/shard_map/ppermute | solution.py:23
  103.8 9.4 %copy-start.6 = (s32[1,64,8]{1,2,0:T(8,128)S(1)}, s32[1,64,8]{1,2,0:T(8,128)}, u32[]{:S(2)}) copy-start(s32[1,64,8]{1,2,0:T(8,128)} %param.13) | copy-start | bytes 6148
  110.0 40.8 %collective-permute-start.17 = (bf16[192,4224]{1,0:T(8,128)(2,1)}, bf16[192,4224]{1,0:T(8,128)(2,1)}, u32[]{:S(2)}, u32[]{:S(2)}) collective-permute-start(bf16[192,4224]{1,0:T(8,128)(2,1)} %pad_maximum_fusion.refs_2_.refs_1_.refs_3_), channel_id=1, source_target_pairs={{0,1},{1,0},{2,3},{3,2},{4,5},{5,4},{6,7},{7,6},{8,9},{9,8},{10,11... | collective-permute-start | bytes 4866056 | tf_op jit(solution)/shard_map/ppermute | solution.py:23
  113.2 142.6 %collective-permute-start.43 = (s32[64,8]{0,1:T(8,128)S(1)}, s32[64,8]{0,1:T(8,128)S(1)}, u32[]{:S(2)}, u32[]{:S(2)}) collective-permute-start(s32[64,8]{0,1:T(8,128)S(1)} %bitcast.32), channel_id=1, source_target_pairs={{0,16},{16,0},{1,17},{17,1},{2,18},{18,2},{3,19},{19,3},{4,20},{20... | collective-permute-start | bytes 6152 | tf_op jit(solution)/shard_map/ppermute | solution.py:491
  122.2 2.2 copy-start.7
  122.2 28.6 %collective-permute-start.14 = (bf16[128,4224]{1,0:T(8,128)(2,1)S(1)}, bf16[128,4224]{1,0:T(8,128)(2,1)S(1)}, u32[]{:S(2)}, u32[]{:S(2)}) collective-permute-start(bf16[128,4224]{1,0:T(8,128)(2,1)S(1)} %pad_maximum_fusion.2.refs_1_.refs_0_.refs_2_), channel_id=1, source_target_pairs={{0,4},{1,5},{2,6},{3,7},{4,0},{5,1},{6,2},{7,3},{8,12},{9,13},{10,... | collective-permute-start | bytes 3244040 | tf_op jit(solution)/shard_map/ppermute | solution.py:23
  150.8 17.7 %copy-start = (bf16[512,1536]{1,0:T(8,128)(2,1)S(1)}, bf16[512,1536]{1,0:T(8,128)(2,1)}, u32[]{:S(2)}) copy-start(bf16[512,1536]{1,0:T(8,128)(2,1)} %get-tuple-element.72.refs_6_) | copy-start | bytes 4718596
  150.8 30.8 %collective-permute-start.22 = (bf16[192,2048]{1,0:T(8,128)(2,1)S(1)}, bf16[192,2048]{1,0:T(8,128)(2,1)}, u32[]{:S(2)}, u32[]{:S(2)}) collective-permute-start(bf16[192,2048]{1,0:T(8,128)(2,1)S(1)} %get-tuple-element.61), channel_id=1, source_target_pairs={{0,1},{1,0},{2,3},{3,2},{4,5},{5,4},{6,7},{7,6},{8,9},{9,8},{10,11... | collective-permute-start | bytes 2359304 | tf_op jit(solution)/shard_map/ppermute | solution.py:23
  151.2 31.7 %collective-permute-start.23 = (bf16[192,2048]{1,0:T(8,128)(2,1)S(1)}, bf16[192,2048]{1,0:T(8,128)(2,1)}, u32[]{:S(2)}, u32[]{:S(2)}) collective-permute-start(bf16[192,2048]{1,0:T(8,128)(2,1)S(1)} %get-tuple-element.62), channel_id=1, source_target_pairs={{0,2},{1,3},{2,0},{3,1},{4,6},{5,7},{6,4},{7,5},{8,10},{9,11},{10,... | collective-permute-start | bytes 2359304 | tf_op jit(solution)/shard_map/ppermute | solution.py:23
  167.0 12.6 %collective-permute-start.21 = (bf16[128,2048]{1,0:T(8,128)(2,1)S(1)}, bf16[128,2048]{1,0:T(8,128)(2,1)S(1)}, u32[]{:S(2)}, u32[]{:S(2)}) collective-permute-start(bf16[128,2048]{1,0:T(8,128)(2,1)S(1)} %get-tuple-element.60), channel_id=1, source_target_pairs={{0,4},{1,5},{2,6},{3,7},{4,0},{5,1},{6,2},{7,3},{8,12},{9,13},{10,... | collective-permute-start | bytes 1572872 | tf_op jit(solution)/shard_map/ppermute | solution.py:23
  168.0 25.0 %collective-permute-start.32 = (bf16[128,2176]{1,0:T(8,128)(2,1)S(1)}, bf16[128,2176]{1,0:T(8,128)(2,1)}, u32[]{:S(2)}, u32[]{:S(2)}) collective-permute-start(bf16[128,2176]{1,0:T(8,128)(2,1)S(1)} %get-tuple-element.63), channel_id=1, source_target_pairs={{0,4},{1,5},{2,6},{3,7},{4,0},{5,1},{6,2},{7,3},{8,12},{9,13},{10,... | collective-permute-start | bytes 1671176 | tf_op jit(solution)/shard_map/ppermute | solution.py:23
  179.6 0.8 copy-start.4
  180.4 3.8 %copy-start.5 = (bf16[128,2048]{1,0:T(8,128)(2,1)S(1)}, bf16[128,2048]{1,0:T(8,128)(2,1)}, u32[]{:S(2)}) copy-start(bf16[128,2048]{1,0:T(8,128)(2,1)} %copy-done.4) | copy-start | bytes 1572868
  180.4 16.0 %collective-permute-start.33 = (bf16[192,2176]{1,0:T(8,128)(2,1)S(1)}, bf16[192,2176]{1,0:T(8,128)(2,1)S(1)}, u32[]{:S(2)}, u32[]{:S(2)}) collective-permute-start(bf16[192,2176]{1,0:T(8,128)(2,1)S(1)} %get-tuple-element.64), channel_id=1, source_target_pairs={{0,1},{1,0},{2,3},{3,2},{4,5},{5,4},{6,7},{7,6},{8,9},{9,8},{10,11... | collective-permute-start | bytes 2506760 | tf_op jit(solution)/shard_map/ppermute | solution.py:23
  181.6 16.7 %collective-permute-start.34 = (bf16[192,2176]{1,0:T(8,128)(2,1)S(1)}, bf16[192,2176]{1,0:T(8,128)(2,1)S(1)}, u32[]{:S(2)}, u32[]{:S(2)}) collective-permute-start(bf16[192,2176]{1,0:T(8,128)(2,1)S(1)} %get-tuple-element.65), channel_id=1, source_target_pairs={{0,2},{1,3},{2,0},{3,1},{4,6},{5,7},{6,4},{7,5},{8,10},{9,11},{10,... | collective-permute-start | bytes 2506760 | tf_op jit(solution)/shard_map/ppermute | solution.py:23
  184.3 19.6 %collective-permute-start.24 = (bf16[64,2048]{1,0:T(8,128)(2,1)S(1)}, bf16[64,2048]{1,0:T(8,128)(2,1)S(1)}, u32[]{:S(2)}, u32[]{:S(2)}) collective-permute-start(bf16[64,2048]{1,0:T(8,128)(2,1)S(1)} %get-tuple-element.88), channel_id=1, source_target_pairs={{0,2},{1,3},{2,0},{3,1},{4,6},{5,7},{6,4},{7,5},{8,10},{9,11},{10,... | collective-permute-start | bytes 786440 | tf_op jit(solution)/shard_map/ppermute | solution.py:23
  193.0 17.0 %collective-permute-start.28 = (bf16[96,2048]{1,0:T(8,128)(2,1)S(1)}, bf16[96,2048]{1,0:T(8,128)(2,1)S(1)}, u32[]{:S(2)}, u32[]{:S(2)}) collective-permute-start(bf16[96,2048]{1,0:T(8,128)(2,1)S(1)} %get-tuple-element.84), channel_id=1, source_target_pairs={{0,1},{1,0},{2,3},{3,2},{4,5},{5,4},{6,7},{7,6},{8,9},{9,8},{10,11... | collective-permute-start | bytes 1179656 | tf_op jit(solution)/shard_map/ppermute | solution.py:23
  196.4 14.2 %collective-permute-start.26 = (bf16[96,2048]{1,0:T(8,128)(2,1)S(1)}, bf16[96,2048]{1,0:T(8,128)(2,1)S(1)}, u32[]{:S(2)}, u32[]{:S(2)}) collective-permute-start(bf16[96,2048]{1,0:T(8,128)(2,1)S(1)} %get-tuple-element.82), channel_id=1, source_target_pairs={{0,4},{1,5},{2,6},{3,7},{4,0},{5,1},{6,2},{7,3},{8,12},{9,13},{10,... | collective-permute-start | bytes 1179656 | tf_op jit(solution)/shard_map/ppermute | solution.py:23
  199.9 10.0 %collective-permute-start.35 = (bf16[64,2176]{1,0:T(8,128)(2,1)S(1)}, bf16[64,2176]{1,0:T(8,128)(2,1)S(1)}, u32[]{:S(2)}, u32[]{:S(2)}) collective-permute-start(bf16[64,2176]{1,0:T(8,128)(2,1)S(1)} %get-tuple-element.86), channel_id=1, source_target_pairs={{0,2},{1,3},{2,0},{3,1},{4,6},{5,7},{6,4},{7,5},{8,10},{9,11},{10,... | collective-permute-start | bytes 835592 | tf_op jit(solution)/shard_map/ppermute | solution.py:23
  203.9 13.3 %collective-permute-start.39 = (bf16[96,2176]{1,0:T(8,128)(2,1)S(1)}, bf16[96,2176]{1,0:T(8,128)(2,1)S(1)}, u32[]{:S(2)}, u32[]{:S(2)}) collective-permute-start(bf16[96,2176]{1,0:T(8,128)(2,1)S(1)} %get-tuple-element.80), channel_id=1, source_target_pairs={{0,1},{1,0},{2,3},{3,2},{4,5},{5,4},{6,7},{7,6},{8,9},{9,8},{10,11... | collective-permute-start | bytes 1253384 | tf_op jit(solution)/shard_map/ppermute | solution.py:23
  209.9 8.6 %collective-permute-start.37 = (bf16[96,2176]{1,0:T(8,128)(2,1)S(1)}, bf16[96,2176]{1,0:T(8,128)(2,1)S(1)}, u32[]{:S(2)}, u32[]{:S(2)}) collective-permute-start(bf16[96,2176]{1,0:T(8,128)(2,1)S(1)} %get-tuple-element.78), channel_id=1, source_target_pairs={{0,4},{1,5},{2,6},{3,7},{4,0},{5,1},{6,2},{7,3},{8,12},{9,13},{10,... | collective-permute-start | bytes 1253384 | tf_op jit(solution)/shard_map/ppermute | solution.py:23
  210.0 6.3 %collective-permute-start.25 = (bf16[32,2048]{1,0:T(8,128)(2,1)S(1)}, bf16[32,2048]{1,0:T(8,128)(2,1)S(1)}, u32[]{:S(2)}, u32[]{:S(2)}) collective-permute-start(bf16[32,2048]{1,0:T(8,128)(2,1)S(1)} %get-tuple-element.104), channel_id=1, source_target_pairs={{0,1},{1,0},{2,3},{3,2},{4,5},{5,4},{6,7},{7,6},{8,9},{9,8},{10,11... | collective-permute-start | bytes 393224 | tf_op jit(solution)/shard_map/ppermute | solution.py:23
  210.7 8.6 %collective-permute-start.36 = (bf16[32,2176]{1,0:T(8,128)(2,1)S(1)}, bf16[32,2176]{1,0:T(8,128)(2,1)S(1)}, u32[]{:S(2)}, u32[]{:S(2)}) collective-permute-start(bf16[32,2176]{1,0:T(8,128)(2,1)S(1)} %get-tuple-element.98), channel_id=1, source_target_pairs={{0,1},{1,0},{2,3},{3,2},{4,5},{5,4},{6,7},{7,6},{8,9},{9,8},{10,11... | collective-permute-start | bytes 417800 | tf_op jit(solution)/shard_map/ppermute | solution.py:23
  216.3 6.9 %collective-permute-start.29 = (bf16[48,2048]{1,0:T(8,128)(2,1)S(1)}, bf16[48,2048]{1,0:T(8,128)(2,1)S(1)}, u32[]{:S(2)}, u32[]{:S(2)}) collective-permute-start(bf16[48,2048]{1,0:T(8,128)(2,1)S(1)} %get-tuple-element.96), channel_id=1, source_target_pairs={{0,4},{1,5},{2,6},{3,7},{4,0},{5,1},{6,2},{7,3},{8,12},{9,13},{10,... | collective-permute-start | bytes 589832 | tf_op jit(solution)/shard_map/ppermute | solution.py:23
  217.2 6.0 %collective-permute-start.27 = (bf16[48,2048]{1,0:T(8,128)(2,1)S(1)}, bf16[48,2048]{1,0:T(8,128)(2,1)S(1)}, u32[]{:S(2)}, u32[]{:S(2)}) collective-permute-start(bf16[48,2048]{1,0:T(8,128)(2,1)S(1)} %get-tuple-element.94), channel_id=1, source_target_pairs={{0,2},{1,3},{2,0},{3,1},{4,6},{5,7},{6,4},{7,5},{8,10},{9,11},{10,... | collective-permute-start | bytes 589832 | tf_op jit(solution)/shard_map/ppermute | solution.py:23
  218.5 13.6 %collective-permute-start.40 = (bf16[48,2176]{1,0:T(8,128)(2,1)S(1)}, bf16[48,2176]{1,0:T(8,128)(2,1)S(1)}, u32[]{:S(2)}, u32[]{:S(2)}) collective-permute-start(bf16[48,2176]{1,0:T(8,128)(2,1)S(1)} %get-tuple-element.92), channel_id=1, source_target_pairs={{0,4},{1,5},{2,6},{3,7},{4,0},{5,1},{6,2},{7,3},{8,12},{9,13},{10,... | collective-permute-start | bytes 626696 | tf_op jit(solution)/shard_map/ppermute | solution.py:23
  219.3 12.9 %collective-permute-start.38 = (bf16[48,2176]{1,0:T(8,128)(2,1)S(1)}, bf16[48,2176]{1,0:T(8,128)(2,1)S(1)}, u32[]{:S(2)}, u32[]{:S(2)}) collective-permute-start(bf16[48,2176]{1,0:T(8,128)(2,1)S(1)} %get-tuple-element.90), channel_id=1, source_target_pairs={{0,2},{1,3},{2,0},{3,1},{4,6},{5,7},{6,4},{7,5},{8,10},{9,11},{10,... | collective-permute-start | bytes 626696 | tf_op jit(solution)/shard_map/ppermute | solution.py:23
  223.4 25.6 %collective-permute-start.31 = (bf16[64,2048]{1,0:T(8,128)(2,1)S(1)}, bf16[64,2048]{1,0:T(8,128)(2,1)S(1)}, u32[]{:S(2)}, u32[]{:S(2)}) collective-permute-start(bf16[64,2048]{1,0:T(8,128)(2,1)S(1)} %pad_maximum_fusion.19), channel_id=1, source_target_pairs={{0,24},{1,25},{2,26},{3,27},{4,28},{5,29},{6,30},{7,31},{8,16},{9,... | collective-permute-start | bytes 786440 | tf_op jit(solution)/shard_map/ppermute | solution.py:84
  232.0 16.9 %collective-permute-start.30 = (bf16[64,2048]{1,0:T(8,128)(2,1)S(1)}, bf16[64,2048]{1,0:T(8,128)(2,1)S(1)}, u32[]{:S(2)}, u32[]{:S(2)}) collective-permute-start(bf16[64,2048]{1,0:T(8,128)(2,1)S(1)} %pad_maximum_fusion.18), channel_id=1, source_target_pairs={{0,16},{1,17},{2,18},{3,19},{4,20},{5,21},{6,22},{7,23},{8,24},{9,... | collective-permute-start | bytes 786440 | tf_op jit(solution)/shard_map/ppermute | solution.py:85
  232.3 22.6 %collective-permute-start.42 = (bf16[64,2176]{1,0:T(8,128)(2,1)S(1)}, bf16[64,2176]{1,0:T(8,128)(2,1)S(1)}, u32[]{:S(2)}, u32[]{:S(2)}) collective-permute-start(bf16[64,2176]{1,0:T(8,128)(2,1)S(1)} %pad_maximum_fusion.16), channel_id=1, source_target_pairs={{0,24},{1,25},{2,26},{3,27},{4,28},{5,29},{6,30},{7,31},{8,16},{9,... | collective-permute-start | bytes 835592 | tf_op jit(solution)/shard_map/ppermute | solution.py:84
  236.2 18.7 %collective-permute-start.41 = (bf16[64,2176]{1,0:T(8,128)(2,1)S(1)}, bf16[64,2176]{1,0:T(8,128)(2,1)S(1)}, u32[]{:S(2)}, u32[]{:S(2)}) collective-permute-start(bf16[64,2176]{1,0:T(8,128)(2,1)S(1)} %pad_maximum_fusion.15), channel_id=1, source_target_pairs={{0,16},{1,17},{2,18},{3,19},{4,20},{5,21},{6,22},{7,23},{8,24},{9,... | collective-permute-start | bytes 835592 | tf_op jit(solution)/shard_map/ppermute | solution.py:85
where the time goes:
time: 261 us; the launch traced here: 256 us
  waiting for transfers between devices  109 us (42%)
  Pallas kernels  70.8 us (27%)
  starting transfers between devices  59.3 us (23%)
  other arithmetic  14 us (5%)
    ppermute x39, waiting for transfers between devices, send(): lax.ppermute(array, 'expert', [(i, i ^ 1 << bit) for i in range(size)])  91.3 us
    ppermute x39, starting transfers between devices, send(): lax.ppermute(array, 'expert', [(i, i ^ 1 << bit) for i in range(size)])  37.7 us
    pallas_call x2, Pallas kernels, back_rows(): pl.pallas_call(lambda *refs: back_kernel(counts, groups, *refs), grid_spe...  31.1 us
    pallas_call x2, Pallas kernels, forward_rows(): pl.pallas_call(lambda *refs: forward_kernel(counts, groups, *refs), grid_...  21.8 us
    pallas_call x2, Pallas kernels, weight_grad(): pl.pallas_call(lambda *refs: weight_kernel(left_counts, right_counts, lef...  17.9 us
    ppermute x2, waiting for transfers between devices, collect_rest(): other = lax.ppermute(other, ('segment', 'expert'), cross(size // 2))  17.9 us
    ppermute x2, starting transfers between devices, collect_rest(): other = lax.ppermute(other, ('segment', 'expert'), cross(size // 2))  12.5 us
    ppermute x1, starting transfers between devices, shards(): other_routes = lax.ppermute(bwd_routes[0], 'segment', swap)  8.93 us
  transfers between devices with their start and end apart: 44, of which 16 were waited for; matrix products, arithmetic and copies ran while one was open for 4% of the time, Pallas kernels for 28%

commit v1 on v0

--- a/solution.py
+++ b/solution.py
@@ -150,9 +150,9 @@
 
 def back_kernel(counts, groups, me_ref, *refs):
     n = len(counts)
-    xd_in, (wgu_ref, wdn_ref) = refs[:n], refs[n : n + 2]
-    dx_out, (dh_out, wa_out) = refs[n + 2 : 2 * n + 2], refs[2 * n + 2 : 2 * n + 4]
-    x, dy, table, wgu, wdn, dx, extra, dh, wa, gate_grad, sems, w_sems, out_sems = refs[2 * n + 4 :]
+    xd_in, tables, (wgu_ref, wdn_ref) = refs[:n], refs[n : 2 * n], refs[2 * n : 2 * n + 2]
+    dx_out, (dh_out, wa_out) = refs[2 * n + 2 : 3 * n + 2], refs[3 * n + 2 : 3 * n + 4]
+    x, dy, table, wgu, wdn, dx, extra, dh, wa, gate_grad, sems, w_sems, out_sems = refs[3 * n + 4 :]
     me = me_ref[0]
     step = pl.program_id(0) if groups > 1 else 0
     ff, width = wdn.shape
@@ -163,7 +163,7 @@
     ins = copies_of(row_pairs(xd_in, x, counts, step, 0, width), sems, 0)
     dys = copies_of(
         row_pairs(xd_in, dy, counts, step, width, width)
-        + row_pairs(xd_in, table, counts, step, 2 * width, lanes),
+        + row_pairs(tables, table, counts, step, width, lanes),
         sems,
         n,
     )
@@ -231,9 +231,9 @@
     return [p.shape[0] // groups for p in pieces]
 
 
-def back_rows(me, xds, w_gu, w_dn, groups):
+def back_rows(me, xds, tables, w_gu, w_dn, groups):
     ff, width = w_dn.shape
-    lanes = xds[0].shape[1] - 2 * width
+    lanes = tables[0].shape[1] - width
     counts = group_counts(xds, groups)
     rows = sum(counts)
     n = len(counts)
@@ -244,7 +244,7 @@
         grid_spec=pltpu.PrefetchScalarGridSpec(
             num_scalar_prefetch=1,
             grid=(groups,),
-            in_specs=[ANY] * (n + 2),
+            in_specs=[ANY] * (2 * n + 2),
             out_specs=[ANY] * (n + 2),
             scratch_shapes=[
                 pltpu.VMEM((rows, width), BF16),
@@ -270,7 +270,7 @@
             bytes_accessed=6 * ff * width + total * (6 * width + 4 * lanes + 6 * ff),
             transcendentals=total * ff,
         ),
-    )(me, *xds, w_gu, w_dn)
+    )(me, *xds, *tables, w_gu, w_dn)
     return out[:n], out[n], out[n + 1]
 
 
@@ -479,7 +479,7 @@
     def forward_last(rows):
         return collect_rest(rows, size, parts).astype(BF16)
 
-    xd_in = jnp.concatenate([bwd_tokens[0], cotangent[0], table], axis=1)
+    xd_in = jnp.concatenate([bwd_tokens[0], cotangent[0]], axis=1)
     if groups > 1:
         y_new = forward_new(after(xf_new, y_kept))
         combined = forward_last(forward_first(y_kept, y_new))
@@ -493,11 +493,11 @@
     if groups == 1:
         y_new = forward_new(after(xf_new, y_kept))
         xd_kept = after(xd_kept, y_new)
-    dx_kept, dh_kept, wa_kept = back_rows(places, xd_kept, w_gu, w_dn, groups)
+    dx_kept, dh_kept, wa_kept = back_rows(places, xd_kept, xf_kept, w_gu, w_dn, groups)
     xd_new = after(xd_new, dx_kept)
     if groups == 1:
         y_new = after(y_new, xd_new)
-    dx_new, dh_new, wa_new = back_rows(places, xd_new, w_gu, w_dn, groups)
+    dx_new, dh_new, wa_new = back_rows(places, xd_new, xf_new, w_gu, w_dn, groups)
     if groups == 1:
         comb_rows = forward_first(y_kept, y_new, dx_new)
         wa_kept = after(wa_kept, comb_rows)

time: 261 us -> 240 us (0.920)
  the two profiles are of different devices: /device:TPU:13 before, /device:TPU:1 now
where the time goes in v1:
time: 240 us
  waiting for transfers between devices  76.7 us (32%)
  Pallas kernels  72.2 us (30%)
  starting transfers between devices  70.3 us (29%)
  other arithmetic  15.2 us (6%)
  local copies, waits for them, and re-layouts  4.23 us (2%)
    ppermute x39, waiting for transfers between devices, send(): lax.ppermute(array, 'expert', [(i, i ^ 1 << bit) for i in range(size)])  59 us
    ppermute x39, starting transfers between devices, send(): lax.ppermute(array, 'expert', [(i, i ^ 1 << bit) for i in range(size)])  46.7 us
    pallas_call x2, Pallas kernels, back_rows(): pl.pallas_call(lambda *refs: back_kernel(counts, groups, *refs), grid_spe...  31.6 us
    pallas_call x2, Pallas kernels, forward_rows(): pl.pallas_call(lambda *refs: forward_kernel(counts, groups, *refs), grid_...  22.4 us
    pallas_call x2, Pallas kernels, weight_grad(): pl.pallas_call(lambda *refs: weight_kernel(left_counts, right_counts, lef...  18.2 us
    ppermute x2, waiting for transfers between devices, collect_rest(): other = lax.ppermute(other, ('segment', 'expert'), cross(size // 2))  17.7 us
    ppermute x2, starting transfers between devices, collect_rest(): other = lax.ppermute(other, ('segment', 'expert'), cross(size // 2))  15.9 us
    ppermute x1, starting transfers between devices, shards(): other_routes = lax.ppermute(bwd_routes[0], 'segment', swap)  7.57 us
  transfers between devices with their start and end apart: 44, of which 17 were waited for; matrix products, arithmetic and copies ran while one was open for 7% of the time, Pallas kernels for 30%

profile of v1, /device:TPU:1, one launch (start us, length us, event | category | flops | bytes accessed | tf_op | source)
XLA Modules:
  0.0 240.0 jit_solution(10058259436538291644)
XLA Ops:
  0.6 3.2 %collective-permute-start = (bf16[64,2048]{1,0:T(8,128)(2,1)}, bf16[64,2048]{1,0:T(8,128)(2,1)S(1)}, u32[]{:S(2)}, u32[]{:S(2)}) collective-permute-start(bf16[64,2048]{1,0:T(8,128)(2,1)} %bitcast.25), channel_id=1, source_target_pairs={{0,8},{1,9},{2,10},{3,11},{4,12},{5,13},{6,14},{7,15},{8,0},{9,1},... | collective-permute-start | bytes 786440 | tf_op jit(solution)/shard_map/ppermute | solution.py:23
  4.5 0.7 select_reduce_fusion.1
  6.0 0.7 select_reduce_fusion.2
  6.9 1.0 pad_maximum_fusion.23
  8.0 1.1 pad_maximum_fusion.8
  9.1 7.0 %collective-permute-done = bf16[64,2048]{1,0:T(8,128)(2,1)S(1)} collective-permute-done((bf16[64,2048]{1,0:T(8,128)(2,1)}, bf16[64,2048]{1,0:T(8,128)(2,1)S(1)}, u32[]{:S(2)}, u32[]{:S(2)}) %collective-permute-start) | collective-permute-done | bytes 262176 | tf_op jit(solution)/shard_map/ppermute | solution.py:23
  16.6 1.1 collective-permute-start.2
  17.7 1.3 collective-permute-start.4
  19.0 4.6 %collective-permute-start.6 = (bf16[48,2176]{1,0:T(8,128)(2,1)S(1)}, bf16[48,2176]{1,0:T(8,128)(2,1)S(1)}, u32[]{:S(2)}, u32[]{:S(2)}) collective-permute-start(bf16[48,2176]{1,0:T(8,128)(2,1)S(1)} %pad_maximum_fusion.21), channel_id=1, source_target_pairs={{0,4},{1,5},{2,6},{3,7},{4,0},{5,1},{6,2},{7,3},{8,12},{9,13},{10,... | collective-permute-start | bytes 626696 | tf_op jit(solution)/shard_map/ppermute | solution.py:23
  23.9 4.1 %collective-permute-start.5 = (bf16[96,2176]{1,0:T(8,128)(2,1)S(1)}, bf16[96,2176]{1,0:T(8,128)(2,1)S(1)}, u32[]{:S(2)}, u32[]{:S(2)}) collective-permute-start(bf16[96,2176]{1,0:T(8,128)(2,1)S(1)} %pad_maximum_fusion.10), channel_id=1, source_target_pairs={{0,4},{1,5},{2,6},{3,7},{4,0},{5,1},{6,2},{7,3},{8,12},{9,13},{10,... | collective-permute-start | bytes 1253384 | tf_op jit(solution)/shard_map/ppermute | solution.py:23
  28.0 3.3 %collective-permute-done.6 = bf16[48,2176]{1,0:T(8,128)(2,1)S(1)} collective-permute-done((bf16[48,2176]{1,0:T(8,128)(2,1)S(1)}, bf16[48,2176]{1,0:T(8,128)(2,1)S(1)}, u32[]{:S(2)}, u32[]{:S(2)}) %collective-permute-start.6) | collective-permute-done | bytes 208928 | tf_op jit(solution)/shard_map/ppermute | solution.py:23
  31.4 0.8 collective-permute-start.7
  32.2 2.3 collective-permute-start.8
  34.5 6.4 %collective-permute-done.11 = bf16[64,4096]{1,0:T(8,128)(2,1)S(1)} collective-permute-done((bf16[64,4096]{1,0:T(8,128)(2,1)S(1)}, bf16[64,4096]{1,0:T(8,128)(2,1)S(1)}, u32[]{:S(2)}, u32[]{:S(2)}) %collective-permute-start.11) | collective-permute-done | bytes 524320 | tf_op jit(solution)/shard_map/ppermute | solution.py:23
  41.0 0.8 collective-permute-start.12
  41.8 1.3 collective-permute-start.15
  43.2 1.3 collective-permute-done.5
  44.5 1.0 collective-permute-start.9
  45.6 1.0 pad_maximum_fusion.4.refs_3_.refs_6_
  46.5 10.9 %shard_map.128 = (bf16[128,2048]{1,0:T(8,128)(2,1)S(1)}, bf16[192,2048]{1,0:T(8,128)(2,1)S(1)}, bf16[192,2048]{1,0:T(8,128)(2,1)S(1)}) custom-call(s32[2]{0:T(128)S(1)} %pad_add_fusion.refs_0_, bf16[128,2176]{1,0:T(8,128)(2,1)S(1)} %pad_maximum_fusion.7.refs_1_.refs_4_, bf16[192,2176]{1,0:T(8,128)(2,1)S(1)} %pad_maximum_fusion.3.refs_2_.refs_5_, ...), custom_call_target="tpu_custom_call" | custom-call | flops 4831838208 | bytes 13631488 | tf_op jit(solution)/shard_map/pallas_call | solution.py:335
  57.5 1.3 collective-permute-start.10
  58.8 6.0 %collective-permute-done.18 = bf16[48,4096]{1,0:T(8,128)(2,1)S(1)} collective-permute-done((bf16[48,4096]{1,0:T(8,128)(2,1)S(1)}, bf16[48,4096]{1,0:T(8,128)(2,1)S(1)}, u32[]{:S(2)}, u32[]{:S(2)}) %collective-permute-start.18) | collective-permute-done | bytes 393248 | tf_op jit(solution)/shard_map/ppermute | solution.py:23
  64.9 1.0 collective-permute-start.19
  66.0 14.9 %collective-permute-done.16 = bf16[96,4096]{1,0:T(8,128)(2,1)S(1)} collective-permute-done((bf16[96,4096]{1,0:T(8,128)(2,1)S(1)}, bf16[96,4096]{1,0:T(8,128)(2,1)S(1)}, u32[]{:S(2)}, u32[]{:S(2)}) %collective-permute-start.16) | collective-permute-done | bytes 786464 | tf_op jit(solution)/shard_map/ppermute | solution.py:23
  80.8 1.0 collective-permute-start.13
  81.9 1.6 collective-permute-start.17
  83.5 1.3 pad_maximum_fusion.1.refs_3_.refs_2_.refs_4_
  84.8 5.0 %collective-permute-done.13 = bf16[64,4096]{1,0:T(8,128)(2,1)S(1)} collective-permute-done((bf16[64,4096]{1,0:T(8,128)(2,1)S(1)}, bf16[64,4096]{1,0:T(8,128)(2,1)S(1)}, u32[]{:S(2)}, u32[]{:S(2)}) %collective-permute-start.13) | collective-permute-done | bytes 524320 | tf_op jit(solution)/shard_map/ppermute | solution.py:23
  89.8 1.1 collective-permute-start.20
  91.0 7.6 %collective-permute-start.43 = (s32[64,8]{0,1:T(8,128)S(1)}, s32[64,8]{0,1:T(8,128)S(1)}, u32[]{:S(2)}, u32[]{:S(2)}) collective-permute-start(s32[64,8]{0,1:T(8,128)S(1)} %bitcast.32), channel_id=1, source_target_pairs={{0,16},{16,0},{1,17},{17,1},{2,18},{18,2},{3,19},{19,3},{4,20},{20... | collective-permute-start | bytes 6152 | tf_op jit(solution)/shard_map/ppermute | solution.py:491
  98.6 0.9 copy-done.13
  99.5 11.5 %shard_map.129 = (bf16[128,2048]{1,0:T(8,128)(2,1)}, bf16[192,2048]{1,0:T(8,128)(2,1)}, bf16[192,2048]{1,0:T(8,128)(2,1)}) custom-call(s32[2]{0:T(128)S(1)} %pad_add_fusion.refs_0_, bf16[128,2176]{1,0:T(8,128)(2,1)S(1)} %collective-permute-done.8.refs_1_.refs_4_, bf16[192,2176]{1,0:T(8,128)(2,1)S(1)} %collective-permute-done.9.refs_2_.refs_5_, ...), custom_call_target="tpu_custom_call" | custom-call | flops 4831838208 | bytes 13631488 | tf_op jit(solution)/shard_map/pallas_call | solution.py:335
  111.0 15.8 %shard_map.130 = (bf16[128,2176]{1,0:T(8,128)(2,1)S(1)}, bf16[192,2176]{1,0:T(8,128)(2,1)S(1)}, bf16[192,2176]{1,0:T(8,128)(2,1)S(1)}, bf16[512,1536]{1,0:T(8,128)(2,1)}, bf16[512,768]{1,0:T(8,128)(2,1)S(1)}) custom-call(s32[2]{0:T(128)S(1)} %pad_add_fusion.refs_0_, bf16[128,4096]{1,0:T(8,128)(2,1)} %copy-done.2, bf16[192,4096]{1,0:T(8,128)(2,1)} %copy-done, ...), custom_call_target="tpu_custom_call" | custom-call | flops 8053063680 | bytes 18350080 | tf_op jit(solution)/shard_map/pallas_call | solution.py:242
  126.9 1.5 collective-permute-start.21
  129.3 15.8 %shard_map.131 = (bf16[128,2176]{1,0:T(8,128)(2,1)S(1)}, bf16[192,2176]{1,0:T(8,128)(2,1)S(1)}, bf16[192,2176]{1,0:T(8,128)(2,1)S(1)}, bf16[512,1536]{1,0:T(8,128)(2,1)}, bf16[512,768]{1,0:T(8,128)(2,1)S(1)}) custom-call(s32[2]{0:T(128)S(1)} %pad_add_fusion.refs_0_, bf16[128,4096]{1,0:T(8,128)(2,1)} %copy-done.4, ...), custom_call_target="tpu_custom_call" | custom-call | flops 8053063680 | bytes 18350080 | tf_op jit(solution)/shard_map/pallas_call | solution.py:242
  145.2 1.2 copy-done.5
  146.5 11.4 %shard_map.132 = bf16[2048,1536]{1,0:T(8,128)(2,1)} custom-call(bf16[128,4096]{1,0:T(8,128)(2,1)S(1)} %copy-done.3, bf16[192,4096]{1,0:T(8,128)(2,1)S(1)} %copy-done.1, bf16[192,4096]{1,0:T(8,128)(2,1)} %pad_maximum_fusion.1.refs_3_.refs_2_.refs_4_, bf16[128,4096]{1,0:T(8,128)(2,1)S(1)} %copy-done.5, ...), custom_call_target="tpu_custom_call" | custom-call | flops 6442450944 | bytes 13631488 | tf_op jit(solution)/shard_map/pallas_call | solution.py:420
  157.9 1.2 collective-permute-start.33
  159.1 0.9 copy-done.10
  160.0 0.9 collective-permute-start.34
  160.9 2.1 add_convert_fusion.5
  163.9 1.2 add_convert_fusion.12
  165.1 6.8 %shard_map.133 = bf16[768,2048]{1,0:T(8,128)(2,1)} custom-call(bf16[512,768]{1,0:T(8,128)(2,1)S(1)} %get-tuple-element.75.refs_0_, bf16[512,768]{1,0:T(8,128)(2,1)S(1)} %get-tuple-element.76.refs_1_, bf16[128,4096]{1,0:T(8,128)(2,1)S(1)} %copy-done.3, bf16[192,4096]{1,0:T(8,128)(2,1)} %copy-done, ...), custom_call_target="tpu_custom_call" | custom-call | flops 3221225472 | bytes 8912896 | tf_op jit(solution)/shard_map/pallas_call | solution.py:420
  171.9 1.5 collective-permute-start.26
  173.5 1.9 collective-permute-start.24
  175.5 0.9 collective-permute-done.34
  176.5 0.8 collective-permute-start.39
  177.7 4.7 %collective-permute-done.24 = bf16[64,2048]{1,0:T(8,128)(2,1)S(1)} collective-permute-done((bf16[64,2048]{1,0:T(8,128)(2,1)S(1)}, bf16[64,2048]{1,0:T(8,128)(2,1)S(1)}, u32[]{:S(2)}, u32[]{:S(2)}) %collective-permute-start.24) | collective-permute-done | bytes 262176 | tf_op jit(solution)/shard_map/ppermute | solution.py:23
  182.3 1.5 collective-permute-start.35
  183.9 5.3 %collective-permute-done.35 = bf16[64,2176]{1,0:T(8,128)(2,1)S(1)} collective-permute-done((bf16[64,2176]{1,0:T(8,128)(2,1)S(1)}, bf16[64,2176]{1,0:T(8,128)(2,1)S(1)}, u32[]{:S(2)}, u32[]{:S(2)}) %collective-permute-start.35) | collective-permute-done | bytes 278560 | tf_op jit(solution)/shard_map/ppermute | solution.py:23
  189.1 4.2 %collective-permute-start.37 = (bf16[96,2176]{1,0:T(8,128)(2,1)S(1)}, bf16[96,2176]{1,0:T(8,128)(2,1)S(1)}, u32[]{:S(2)}, u32[]{:S(2)}) collective-permute-start(bf16[96,2176]{1,0:T(8,128)(2,1)S(1)} %get-tuple-element.78), channel_id=1, source_target_pairs={{0,4},{1,5},{2,6},{3,7},{4,0},{5,1},{6,2},{7,3},{8,12},{9,13},{10,... | collective-permute-start | bytes 1253384 | tf_op jit(solution)/shard_map/ppermute | solution.py:23
  193.5 1.1 add_convert_fusion.18
  194.7 1.5 collective-permute-start.36
  196.3 1.1 collective-permute-done.25
  197.4 1.4 collective-permute-start.29
  199.5 0.9 collective-permute-start.40
  200.9 2.0 collective-permute-done.29
  202.9 0.8 collective-permute-done.27
  203.8 12.1 %collective-permute-start.31 = (bf16[64,2048]{1,0:T(8,128)(2,1)S(1)}, bf16[64,2048]{1,0:T(8,128)(2,1)S(1)}, u32[]{:S(2)}, u32[]{:S(2)}) collective-permute-start(bf16[64,2048]{1,0:T(8,128)(2,1)S(1)} %pad_maximum_fusion.19), channel_id=1, source_target_pairs={{0,24},{1,25},{2,26},{3,27},{4,28},{5,29},{6,30},{7,31},{8,16},{9,... | collective-permute-start | bytes 786440 | tf_op jit(solution)/shard_map/ppermute | solution.py:84
  216.1 3.9 %collective-permute-start.42 = (bf16[64,2176]{1,0:T(8,128)(2,1)S(1)}, bf16[64,2176]{1,0:T(8,128)(2,1)S(1)}, u32[]{:S(2)}, u32[]{:S(2)}) collective-permute-start(bf16[64,2176]{1,0:T(8,128)(2,1)S(1)} %pad_maximum_fusion.16), channel_id=1, source_target_pairs={{0,24},{1,25},{2,26},{3,27},{4,28},{5,29},{6,30},{7,31},{8,16},{9,... | collective-permute-start | bytes 835592 | tf_op jit(solution)/shard_map/ppermute | solution.py:84
  220.1 14.0 %collective-permute-done.31 = bf16[64,2048]{1,0:T(8,128)(2,1)S(1)} collective-permute-done((bf16[64,2048]{1,0:T(8,128)(2,1)S(1)}, bf16[64,2048]{1,0:T(8,128)(2,1)S(1)}, u32[]{:S(2)}, u32[]{:S(2)}) %collective-permute-start.31) | collective-permute-done | bytes 262176 | tf_op jit(solution)/shard_map/ppermute | solution.py:84
  234.1 0.8 fusion
  234.9 3.7 %collective-permute-done.42 = bf16[64,2176]{1,0:T(8,128)(2,1)S(1)} collective-permute-done((bf16[64,2176]{1,0:T(8,128)(2,1)S(1)}, bf16[64,2176]{1,0:T(8,128)(2,1)S(1)}, u32[]{:S(2)}, u32[]{:S(2)}) %collective-permute-start.42) | collective-permute-done | bytes 278560 | tf_op jit(solution)/shard_map/ppermute | solution.py:84
  238.6 0.7 fusion.1
  (123 shorter events, 8.6 us)
Async XLA Ops:
  0.6 8.4 %copy-start.8 = (bf16[1,64,2048]{2,1,0:T(8,128)(2,1)S(1)}, bf16[1,64,2048]{2,1,0:T(8,128)(2,1)}, u32[]{:S(2)}) copy-start(bf16[1,64,2048]{2,1,0:T(8,128)(2,1)} %param.9) | copy-start | bytes 786436
  0.6 15.4 %collective-permute-start = (bf16[64,2048]{1,0:T(8,128)(2,1)}, bf16[64,2048]{1,0:T(8,128)(2,1)S(1)}, u32[]{:S(2)}, u32[]{:S(2)}) collective-permute-start(bf16[64,2048]{1,0:T(8,128)(2,1)} %bitcast.25), channel_id=1, source_target_pairs={{0,8},{1,9},{2,10},{3,11},{4,12},{5,13},{6,14},{7,15},{8,0},{9,1},... | collective-permute-start | bytes 786440 | tf_op jit(solution)/shard_map/ppermute | solution.py:23
  6.9 9.5 %collective-permute-start.1 = (bf16[64,128]{1,0:T(8,128)(2,1)S(1)}, bf16[64,128]{1,0:T(8,128)(2,1)S(1)}, u32[]{:S(2)}, u32[]{:S(2)}) collective-permute-start(bf16[64,128]{1,0:T(8,128)(2,1)S(1)} %fusion.4), channel_id=1, source_target_pairs={{0,8},{1,9},{2,10},{3,11},{4,12},{5,13},{6,14},{7,15},{8,0},{9,1},... | collective-permute-start | bytes 49160 | tf_op jit(solution)/shard_map/ppermute | solution.py:23
  16.4 24.5 %collective-permute-start.11 = (bf16[64,4096]{1,0:T(8,128)(2,1)S(1)}, bf16[64,4096]{1,0:T(8,128)(2,1)S(1)}, u32[]{:S(2)}, u32[]{:S(2)}) collective-permute-start(bf16[64,4096]{1,0:T(8,128)(2,1)S(1)} %pad_maximum_fusion.8), channel_id=1, source_target_pairs={{0,8},{1,9},{2,10},{3,11},{4,12},{5,13},{6,14},{7,15},{8,0},{9,1},... | collective-permute-start | bytes 1572872 | tf_op jit(solution)/shard_map/ppermute | solution.py:23
  16.6 7.0 %collective-permute-start.2 = (bf16[32,2176]{1,0:T(8,128)(2,1)S(1)}, bf16[32,2176]{1,0:T(8,128)(2,1)S(1)}, u32[]{:S(2)}, u32[]{:S(2)}) collective-permute-start(bf16[32,2176]{1,0:T(8,128)(2,1)S(1)} %pad_maximum_fusion.22), channel_id=1, source_target_pairs={{0,1},{1,0},{2,3},{3,2},{4,5},{5,4},{6,7},{7,6},{8,9},{9,8},{10,11... | collective-permute-start | bytes 417800 | tf_op jit(solution)/shard_map/ppermute | solution.py:23
  17.7 6.2 %collective-permute-start.4 = (bf16[48,2176]{1,0:T(8,128)(2,1)S(1)}, bf16[48,2176]{1,0:T(8,128)(2,1)S(1)}, u32[]{:S(2)}, u32[]{:S(2)}) collective-permute-start(bf16[48,2176]{1,0:T(8,128)(2,1)S(1)} %pad_maximum_fusion.20), channel_id=1, source_target_pairs={{0,2},{1,3},{2,0},{3,1},{4,6},{5,7},{6,4},{7,5},{8,10},{9,11},{10,... | collective-permute-start | bytes 626696 | tf_op jit(solution)/shard_map/ppermute | solution.py:23
  19.0 12.3 %collective-permute-start.6 = (bf16[48,2176]{1,0:T(8,128)(2,1)S(1)}, bf16[48,2176]{1,0:T(8,128)(2,1)S(1)}, u32[]{:S(2)}, u32[]{:S(2)}) collective-permute-start(bf16[48,2176]{1,0:T(8,128)(2,1)S(1)} %pad_maximum_fusion.21), channel_id=1, source_target_pairs={{0,4},{1,5},{2,6},{3,7},{4,0},{5,1},{6,2},{7,3},{8,12},{9,13},{10,... | collective-permute-start | bytes 626696 | tf_op jit(solution)/shard_map/ppermute | solution.py:23
  23.6 8.6 %collective-permute-start.3 = (bf16[64,2176]{1,0:T(8,128)(2,1)S(1)}, bf16[64,2176]{1,0:T(8,128)(2,1)S(1)}, u32[]{:S(2)}, u32[]{:S(2)}) collective-permute-start(bf16[64,2176]{1,0:T(8,128)(2,1)S(1)} %pad_maximum_fusion.14), channel_id=1, source_target_pairs={{0,2},{1,3},{2,0},{3,1},{4,6},{5,7},{6,4},{7,5},{8,10},{9,11},{10,... | collective-permute-start | bytes 835592 | tf_op jit(solution)/shard_map/ppermute | solution.py:23
  23.9 20.5 %collective-permute-start.5 = (bf16[96,2176]{1,0:T(8,128)(2,1)S(1)}, bf16[96,2176]{1,0:T(8,128)(2,1)S(1)}, u32[]{:S(2)}, u32[]{:S(2)}) collective-permute-start(bf16[96,2176]{1,0:T(8,128)(2,1)S(1)} %pad_maximum_fusion.10), channel_id=1, source_target_pairs={{0,4},{1,5},{2,6},{3,7},{4,0},{5,1},{6,2},{7,3},{8,12},{9,13},{10,... | collective-permute-start | bytes 1253384 | tf_op jit(solution)/shard_map/ppermute | solution.py:23
  31.4 13.2 %collective-permute-start.7 = (bf16[96,2176]{1,0:T(8,128)(2,1)S(1)}, bf16[96,2176]{1,0:T(8,128)(2,1)S(1)}, u32[]{:S(2)}, u32[]{:S(2)}) collective-permute-start(bf16[96,2176]{1,0:T(8,128)(2,1)S(1)} %pad_maximum_fusion.11), channel_id=1, source_target_pairs={{0,1},{1,0},{2,3},{3,2},{4,5},{5,4},{6,7},{7,6},{8,9},{9,8},{10,11... | collective-permute-start | bytes 1253384 | tf_op jit(solution)/shard_map/ppermute | solution.py:23
  32.2 58.7 %collective-permute-start.8 = (bf16[128,2176]{1,0:T(8,128)(2,1)S(1)}, bf16[128,2176]{1,0:T(8,128)(2,1)S(1)}, u32[]{:S(2)}, u32[]{:S(2)}) collective-permute-start(bf16[128,2176]{1,0:T(8,128)(2,1)S(1)} %pad_maximum_fusion.7.refs_1_.refs_4_), channel_id=1, source_target_pairs={{0,4},{1,5},{2,6},{3,7},{4,0},{5,1},{6,2},{7,3},{8,12},{9,13},{10,... | collective-permute-start | bytes 1671176 | tf_op jit(solution)/shard_map/ppermute | solution.py:23
  41.0 23.9 %collective-permute-start.12 = (bf16[32,4096]{1,0:T(8,128)(2,1)S(1)}, bf16[32,4096]{1,0:T(8,128)(2,1)S(1)}, u32[]{:S(2)}, u32[]{:S(2)}) collective-permute-start(bf16[32,4096]{1,0:T(8,128)(2,1)S(1)} %pad_maximum_fusion.17), channel_id=1, source_target_pairs={{0,1},{1,0},{2,3},{3,2},{4,5},{5,4},{6,7},{7,6},{8,9},{9,8},{10,11... | collective-permute-start | bytes 786440 | tf_op jit(solution)/shard_map/ppermute | solution.py:23
  41.8 15.6 %collective-permute-start.15 = (bf16[48,4096]{1,0:T(8,128)(2,1)S(1)}, bf16[48,4096]{1,0:T(8,128)(2,1)S(1)}, u32[]{:S(2)}, u32[]{:S(2)}) collective-permute-start(bf16[48,4096]{1,0:T(8,128)(2,1)S(1)} %pad_maximum_fusion.12), channel_id=1, source_target_pairs={{0,2},{1,3},{2,0},{3,1},{4,6},{5,7},{6,4},{7,5},{8,10},{9,11},{10,... | collective-permute-start | bytes 1179656 | tf_op jit(solution)/shard_map/ppermute | solution.py:23
  44.5 20.4 %collective-permute-start.18 = (bf16[48,4096]{1,0:T(8,128)(2,1)S(1)}, bf16[48,4096]{1,0:T(8,128)(2,1)S(1)}, u32[]{:S(2)}, u32[]{:S(2)}) collective-permute-start(bf16[48,4096]{1,0:T(8,128)(2,1)S(1)} %pad_maximum_fusion.13), channel_id=1, source_target_pairs={{0,4},{1,5},{2,6},{3,7},{4,0},{5,1},{6,2},{7,3},{8,12},{9,13},{10,... | collective-permute-start | bytes 1179656 | tf_op jit(solution)/shard_map/ppermute | solution.py:23
  44.5 12.9 %copy-start.6 = (bf16[192,2176]{1,0:T(8,128)(2,1)}, bf16[192,2176]{1,0:T(8,128)(2,1)S(1)}, u32[]{:S(2)}) copy-start(bf16[192,2176]{1,0:T(8,128)(2,1)S(1)} %pad_maximum_fusion.3.refs_2_.refs_5_) | copy-start | bytes 2506756
  44.5 54.0 %collective-permute-start.9 = (bf16[192,2176]{1,0:T(8,128)(2,1)S(1)}, bf16[192,2176]{1,0:T(8,128)(2,1)S(1)}, u32[]{:S(2)}, u32[]{:S(2)}) collective-permute-start(bf16[192,2176]{1,0:T(8,128)(2,1)S(1)} %pad_maximum_fusion.3.refs_2_.refs_5_), channel_id=1, source_target_pairs={{0,1},{1,0},{2,3},{3,2},{4,5},{5,4},{6,7},{7,6},{8,9},{9,8},{10,11... | collective-permute-start | bytes 2506760 | tf_op jit(solution)/shard_map/ppermute | solution.py:23
  46.5 10.9 %copy-start.9 = (bf16[192,2176]{1,0:T(8,128)(2,1)S(1)}, bf16[192,2176]{1,0:T(8,128)(2,1)}, u32[]{:S(2)}) copy-start(bf16[192,2176]{1,0:T(8,128)(2,1)} %pad_maximum_fusion.4.refs_3_.refs_6_) | copy-start | bytes 2506756
  57.5 41.1 %collective-permute-start.10 = (bf16[192,2176]{1,0:T(8,128)(2,1)S(1)}, bf16[192,2176]{1,0:T(8,128)(2,1)S(1)}, u32[]{:S(2)}, u32[]{:S(2)}) collective-permute-start(bf16[192,2176]{1,0:T(8,128)(2,1)S(1)} %copy-done.9), channel_id=1, source_target_pairs={{0,2},{1,3},{2,0},{3,1},{4,6},{5,7},{6,4},{7,5},{8,10},{9,11},{10,... | collective-permute-start | bytes 2506760 | tf_op jit(solution)/shard_map/ppermute | solution.py:23
  64.8 16.0 %collective-permute-start.16 = (bf16[96,4096]{1,0:T(8,128)(2,1)S(1)}, bf16[96,4096]{1,0:T(8,128)(2,1)S(1)}, u32[]{:S(2)}, u32[]{:S(2)}) collective-permute-start(bf16[96,4096]{1,0:T(8,128)(2,1)S(1)} %pad_maximum_fusion.5), channel_id=1, source_target_pairs={{0,4},{1,5},{2,6},{3,7},{4,0},{5,1},{6,2},{7,3},{8,12},{9,13},{10,... | collective-permute-start | bytes 2359304 | tf_op jit(solution)/shard_map/ppermute | solution.py:23
  64.9 17.0 %collective-permute-start.19 = (bf16[96,4096]{1,0:T(8,128)(2,1)S(1)}, bf16[96,4096]{1,0:T(8,128)(2,1)S(1)}, u32[]{:S(2)}, u32[]{:S(2)}) collective-permute-start(bf16[96,4096]{1,0:T(8,128)(2,1)S(1)} %pad_maximum_fusion.6), channel_id=1, source_target_pairs={{0,1},{1,0},{2,3},{3,2},{4,5},{5,4},{6,7},{7,6},{8,9},{9,8},{10,11... | collective-permute-start | bytes 2359304 | tf_op jit(solution)/shard_map/ppermute | solution.py:23
  80.8 9.0 %collective-permute-start.13 = (bf16[64,4096]{1,0:T(8,128)(2,1)S(1)}, bf16[64,4096]{1,0:T(8,128)(2,1)S(1)}, u32[]{:S(2)}, u32[]{:S(2)}) collective-permute-start(bf16[64,4096]{1,0:T(8,128)(2,1)S(1)} %pad_maximum_fusion.9), channel_id=1, source_target_pairs={{0,2},{1,3},{2,0},{3,1},{4,6},{5,7},{6,4},{7,5},{8,10},{9,11},{10,... | collective-permute-start | bytes 1572872 | tf_op jit(solution)/shard_map/ppermute | solution.py:23
  81.9 9.0 %copy-start = (bf16[192,4096]{1,0:T(8,128)(2,1)}, bf16[192,4096]{1,0:T(8,128)(2,1)S(1)}, u32[]{:S(2)}) copy-start(bf16[192,4096]{1,0:T(8,128)(2,1)S(1)} %pad_maximum_fusion.refs_2_.refs_1_.refs_3_) | copy-start | bytes 4718596
  81.9 44.9 %collective-permute-start.17 = (bf16[192,4096]{1,0:T(8,128)(2,1)S(1)}, bf16[192,4096]{1,0:T(8,128)(2,1)}, u32[]{:S(2)}, u32[]{:S(2)}) collective-permute-start(bf16[192,4096]{1,0:T(8,128)(2,1)S(1)} %pad_maximum_fusion.refs_2_.refs_1_.refs_3_), channel_id=1, source_target_pairs={{0,1},{1,0},{2,3},{3,2},{4,5},{5,4},{6,7},{7,6},{8,9},{9,8},{10,11... | collective-permute-start | bytes 4718600 | tf_op jit(solution)/shard_map/ppermute | solution.py:23
  84.8 6.2 %copy-start.12 = (s32[1,64,8]{1,2,0:T(8,128)S(1)}, s32[1,64,8]{1,2,0:T(8,128)}, u32[]{:S(2)}) copy-start(s32[1,64,8]{1,2,0:T(8,128)} %param.13) | copy-start | bytes 6148
  89.8 37.1 %collective-permute-start.20 = (bf16[192,4096]{1,0:T(8,128)(2,1)}, bf16[192,4096]{1,0:T(8,128)(2,1)}, u32[]{:S(2)}, u32[]{:S(2)}) collective-permute-start(bf16[192,4096]{1,0:T(8,128)(2,1)} %pad_maximum_fusion.1.refs_3_.refs_2_.refs_4_), channel_id=1, source_target_pairs={{0,2},{1,3},{2,0},{3,1},{4,6},{5,7},{6,4},{7,5},{8,10},{9,11},{10,... | collective-permute-start | bytes 4718600 | tf_op jit(solution)/shard_map/ppermute | solution.py:23
  90.9 20.0 %copy-start.2 = (bf16[128,4096]{1,0:T(8,128)(2,1)}, bf16[128,4096]{1,0:T(8,128)(2,1)S(1)}, u32[]{:S(2)}) copy-start(bf16[128,4096]{1,0:T(8,128)(2,1)S(1)} %pad_maximum_fusion.2.refs_1_.refs_0_.refs_2_) | copy-start | bytes 3145732
  91.0 148.4 %collective-permute-start.43 = (s32[64,8]{0,1:T(8,128)S(1)}, s32[64,8]{0,1:T(8,128)S(1)}, u32[]{:S(2)}, u32[]{:S(2)}) collective-permute-start(s32[64,8]{0,1:T(8,128)S(1)} %bitcast.32), channel_id=1, source_target_pairs={{0,16},{16,0},{1,17},{17,1},{2,18},{18,2},{3,19},{19,3},{4,20},{20... | collective-permute-start | bytes 6152 | tf_op jit(solution)/shard_map/ppermute | solution.py:491
  98.6 12.5 %copy-start.7 = (bf16[192,2176]{1,0:T(8,128)(2,1)}, bf16[192,2176]{1,0:T(8,128)(2,1)S(1)}, u32[]{:S(2)}) copy-start(bf16[192,2176]{1,0:T(8,128)(2,1)S(1)} %collective-permute-done.9.refs_2_.refs_5_) | copy-start | bytes 2506756
  98.6 28.3 %collective-permute-start.14 = (bf16[128,4096]{1,0:T(8,128)(2,1)S(1)}, bf16[128,4096]{1,0:T(8,128)(2,1)S(1)}, u32[]{:S(2)}, u32[]{:S(2)}) collective-permute-start(bf16[128,4096]{1,0:T(8,128)(2,1)S(1)} %pad_maximum_fusion.2.refs_1_.refs_0_.refs_2_), channel_id=1, source_target_pairs={{0,4},{1,5},{2,6},{3,7},{4,0},{5,1},{6,2},{7,3},{8,12},{9,13},{10,... | collective-permute-start | bytes 3145736 | tf_op jit(solution)/shard_map/ppermute | solution.py:23
  98.6 1.0 copy-start.13
  126.9 2.4 %copy-start.4 = (bf16[128,4096]{1,0:T(8,128)(2,1)}, bf16[128,4096]{1,0:T(8,128)(2,1)S(1)}, u32[]{:S(2)}) copy-start(bf16[128,4096]{1,0:T(8,128)(2,1)S(1)} %collective-permute-done.14.refs_1_.refs_3_.refs_5_) | copy-start | bytes 3145732
  126.9 18.4 %copy-start.1 = (bf16[192,4096]{1,0:T(8,128)(2,1)S(1)}, bf16[192,4096]{1,0:T(8,128)(2,1)}, u32[]{:S(2)}) copy-start(bf16[192,4096]{1,0:T(8,128)(2,1)} %copy-done) | copy-start | bytes 4718596
  126.9 18.4 %copy-start.3 = (bf16[128,4096]{1,0:T(8,128)(2,1)S(1)}, bf16[128,4096]{1,0:T(8,128)(2,1)}, u32[]{:S(2)}) copy-start(bf16[128,4096]{1,0:T(8,128)(2,1)} %copy-done.2) | copy-start | bytes 3145732
  126.9 31.0 %collective-permute-start.21 = (bf16[128,2048]{1,0:T(8,128)(2,1)}, bf16[128,2048]{1,0:T(8,128)(2,1)}, u32[]{:S(2)}, u32[]{:S(2)}) collective-permute-start(bf16[128,2048]{1,0:T(8,128)(2,1)} %get-tuple-element.60), channel_id=1, source_target_pairs={{0,4},{1,5},{2,6},{3,7},{4,0},{5,1},{6,2},{7,3},{8,12},{9,13},{10,... | collective-permute-start | bytes 1572872 | tf_op jit(solution)/shard_map/ppermute | solution.py:23
  128.4 30.7 %collective-permute-start.22 = (bf16[192,2048]{1,0:T(8,128)(2,1)}, bf16[192,2048]{1,0:T(8,128)(2,1)S(1)}, u32[]{:S(2)}, u32[]{:S(2)}) collective-permute-start(bf16[192,2048]{1,0:T(8,128)(2,1)} %get-tuple-element.61), channel_id=1, source_target_pairs={{0,1},{1,0},{2,3},{3,2},{4,5},{5,4},{6,7},{7,6},{8,9},{9,8},{10,11... | collective-permute-start | bytes 2359304 | tf_op jit(solution)/shard_map/ppermute | solution.py:23
  129.0 31.9 %collective-permute-start.23 = (bf16[192,2048]{1,0:T(8,128)(2,1)}, bf16[192,2048]{1,0:T(8,128)(2,1)}, u32[]{:S(2)}, u32[]{:S(2)}) collective-permute-start(bf16[192,2048]{1,0:T(8,128)(2,1)} %get-tuple-element.62), channel_id=1, source_target_pairs={{0,2},{1,3},{2,0},{3,1},{4,6},{5,7},{6,4},{7,5},{8,10},{9,11},{10,... | collective-permute-start | bytes 2359304 | tf_op jit(solution)/shard_map/ppermute | solution.py:23
  145.1 26.8 %collective-permute-start.32 = (bf16[128,2176]{1,0:T(8,128)(2,1)S(1)}, bf16[128,2176]{1,0:T(8,128)(2,1)S(1)}, u32[]{:S(2)}, u32[]{:S(2)}) collective-permute-start(bf16[128,2176]{1,0:T(8,128)(2,1)S(1)} %get-tuple-element.63), channel_id=1, source_target_pairs={{0,4},{1,5},{2,6},{3,7},{4,0},{5,1},{6,2},{7,3},{8,12},{9,13},{10,... | collective-permute-start | bytes 1671176 | tf_op jit(solution)/shard_map/ppermute | solution.py:23
  145.2 1.2 copy-start.5
  157.9 15.6 %collective-permute-start.33 = (bf16[192,2176]{1,0:T(8,128)(2,1)S(1)}, bf16[192,2176]{1,0:T(8,128)(2,1)S(1)}, u32[]{:S(2)}, u32[]{:S(2)}) collective-permute-start(bf16[192,2176]{1,0:T(8,128)(2,1)S(1)} %get-tuple-element.64), channel_id=1, source_target_pairs={{0,1},{1,0},{2,3},{3,2},{4,5},{5,4},{6,7},{7,6},{8,9},{9,8},{10,11... | collective-permute-start | bytes 2506760 | tf_op jit(solution)/shard_map/ppermute | solution.py:23
  159.1 0.9 copy-start.10
  160.0 3.7 %copy-start.11 = (bf16[192,2048]{1,0:T(8,128)(2,1)S(1)}, bf16[192,2048]{1,0:T(8,128)(2,1)}, u32[]{:S(2)}) copy-start(bf16[192,2048]{1,0:T(8,128)(2,1)} %copy-done.10) | copy-start | bytes 2359300
  160.0 16.3 %collective-permute-start.34 = (bf16[192,2176]{1,0:T(8,128)(2,1)S(1)}, bf16[192,2176]{1,0:T(8,128)(2,1)S(1)}, u32[]{:S(2)}, u32[]{:S(2)}) collective-permute-start(bf16[192,2176]{1,0:T(8,128)(2,1)S(1)} %get-tuple-element.65), channel_id=1, source_target_pairs={{0,2},{1,3},{2,0},{3,1},{4,6},{5,7},{6,4},{7,5},{8,10},{9,11},{10,... | collective-permute-start | bytes 2506760 | tf_op jit(solution)/shard_map/ppermute | solution.py:23
  163.0 30.4 %collective-permute-start.28 = (bf16[96,2048]{1,0:T(8,128)(2,1)}, bf16[96,2048]{1,0:T(8,128)(2,1)}, u32[]{:S(2)}, u32[]{:S(2)}) collective-permute-start(bf16[96,2048]{1,0:T(8,128)(2,1)} %get-tuple-element.84), channel_id=1, source_target_pairs={{0,1},{1,0},{2,3},{3,2},{4,5},{5,4},{6,7},{7,6},{8,9},{9,8},{10,11... | collective-permute-start | bytes 1179656 | tf_op jit(solution)/shard_map/ppermute | solution.py:23
  171.9 22.7 %collective-permute-start.26 = (bf16[96,2048]{1,0:T(8,128)(2,1)S(1)}, bf16[96,2048]{1,0:T(8,128)(2,1)S(1)}, u32[]{:S(2)}, u32[]{:S(2)}) collective-permute-start(bf16[96,2048]{1,0:T(8,128)(2,1)S(1)} %get-tuple-element.82), channel_id=1, source_target_pairs={{0,4},{1,5},{2,6},{3,7},{4,0},{5,1},{6,2},{7,3},{8,12},{9,13},{10,... | collective-permute-start | bytes 1179656 | tf_op jit(solution)/shard_map/ppermute | solution.py:23
  173.5 8.8 %collective-permute-start.24 = (bf16[64,2048]{1,0:T(8,128)(2,1)S(1)}, bf16[64,2048]{1,0:T(8,128)(2,1)S(1)}, u32[]{:S(2)}, u32[]{:S(2)}) collective-permute-start(bf16[64,2048]{1,0:T(8,128)(2,1)S(1)} %get-tuple-element.88), channel_id=1, source_target_pairs={{0,2},{1,3},{2,0},{3,1},{4,6},{5,7},{6,4},{7,5},{8,10},{9,11},{10,... | collective-permute-start | bytes 786440 | tf_op jit(solution)/shard_map/ppermute | solution.py:23
  176.5 22.3 %collective-permute-start.39 = (bf16[96,2176]{1,0:T(8,128)(2,1)S(1)}, bf16[96,2176]{1,0:T(8,128)(2,1)S(1)}, u32[]{:S(2)}, u32[]{:S(2)}) collective-permute-start(bf16[96,2176]{1,0:T(8,128)(2,1)S(1)} %get-tuple-element.80), channel_id=1, source_target_pairs={{0,1},{1,0},{2,3},{3,2},{4,5},{5,4},{6,7},{7,6},{8,9},{9,8},{10,11... | collective-permute-start | bytes 1253384 | tf_op jit(solution)/shard_map/ppermute | solution.py:23
  182.3 6.8 %collective-permute-start.35 = (bf16[64,2176]{1,0:T(8,128)(2,1)S(1)}, bf16[64,2176]{1,0:T(8,128)(2,1)S(1)}, u32[]{:S(2)}, u32[]{:S(2)}) collective-permute-start(bf16[64,2176]{1,0:T(8,128)(2,1)S(1)} %get-tuple-element.86), channel_id=1, source_target_pairs={{0,2},{1,3},{2,0},{3,1},{4,6},{5,7},{6,4},{7,5},{8,10},{9,11},{10,... | collective-permute-start | bytes 835592 | tf_op jit(solution)/shard_map/ppermute | solution.py:23
  189.1 10.3 %collective-permute-start.37 = (bf16[96,2176]{1,0:T(8,128)(2,1)S(1)}, bf16[96,2176]{1,0:T(8,128)(2,1)S(1)}, u32[]{:S(2)}, u32[]{:S(2)}) collective-permute-start(bf16[96,2176]{1,0:T(8,128)(2,1)S(1)} %get-tuple-element.78), channel_id=1, source_target_pairs={{0,4},{1,5},{2,6},{3,7},{4,0},{5,1},{6,2},{7,3},{8,12},{9,13},{10,... | collective-permute-start | bytes 1253384 | tf_op jit(solution)/shard_map/ppermute | solution.py:23
  193.5 3.9 %collective-permute-start.25 = (bf16[32,2048]{1,0:T(8,128)(2,1)S(1)}, bf16[32,2048]{1,0:T(8,128)(2,1)S(1)}, u32[]{:S(2)}, u32[]{:S(2)}) collective-permute-start(bf16[32,2048]{1,0:T(8,128)(2,1)S(1)} %get-tuple-element.100), channel_id=1, source_target_pairs={{0,1},{1,0},{2,3},{3,2},{4,5},{5,4},{6,7},{7,6},{8,9},{9,8},{10,11... | collective-permute-start | bytes 393224 | tf_op jit(solution)/shard_map/ppermute | solution.py:23
  194.7 5.8 %collective-permute-start.36 = (bf16[32,2176]{1,0:T(8,128)(2,1)S(1)}, bf16[32,2176]{1,0:T(8,128)(2,1)S(1)}, u32[]{:S(2)}, u32[]{:S(2)}) collective-permute-start(bf16[32,2176]{1,0:T(8,128)(2,1)S(1)} %get-tuple-element.98), channel_id=1, source_target_pairs={{0,1},{1,0},{2,3},{3,2},{4,5},{5,4},{6,7},{7,6},{8,9},{9,8},{10,11... | collective-permute-start | bytes 417800 | tf_op jit(solution)/shard_map/ppermute | solution.py:23
  197.4 5.5 %collective-permute-start.29 = (bf16[48,2048]{1,0:T(8,128)(2,1)S(1)}, bf16[48,2048]{1,0:T(8,128)(2,1)S(1)}, u32[]{:S(2)}, u32[]{:S(2)}) collective-permute-start(bf16[48,2048]{1,0:T(8,128)(2,1)S(1)} %get-tuple-element.96), channel_id=1, source_target_pairs={{0,4},{1,5},{2,6},{3,7},{4,0},{5,1},{6,2},{7,3},{8,12},{9,13},{10,... | collective-permute-start | bytes 589832 | tf_op jit(solution)/shard_map/ppermute | solution.py:23
  198.8 4.9 %collective-permute-start.27 = (bf16[48,2048]{1,0:T(8,128)(2,1)S(1)}, bf16[48,2048]{1,0:T(8,128)(2,1)S(1)}, u32[]{:S(2)}, u32[]{:S(2)}) collective-permute-start(bf16[48,2048]{1,0:T(8,128)(2,1)S(1)} %get-tuple-element.94), channel_id=1, source_target_pairs={{0,2},{1,3},{2,0},{3,1},{4,6},{5,7},{6,4},{7,5},{8,10},{9,11},{10,... | collective-permute-start | bytes 589832 | tf_op jit(solution)/shard_map/ppermute | solution.py:23
  199.5 16.5 %collective-permute-start.40 = (bf16[48,2176]{1,0:T(8,128)(2,1)S(1)}, bf16[48,2176]{1,0:T(8,128)(2,1)S(1)}, u32[]{:S(2)}, u32[]{:S(2)}) collective-permute-start(bf16[48,2176]{1,0:T(8,128)(2,1)S(1)} %get-tuple-element.92), channel_id=1, source_target_pairs={{0,4},{1,5},{2,6},{3,7},{4,0},{5,1},{6,2},{7,3},{8,12},{9,13},{10,... | collective-permute-start | bytes 626696 | tf_op jit(solution)/shard_map/ppermute | solution.py:23
  200.4 15.6 %collective-permute-start.38 = (bf16[48,2176]{1,0:T(8,128)(2,1)S(1)}, bf16[48,2176]{1,0:T(8,128)(2,1)S(1)}, u32[]{:S(2)}, u32[]{:S(2)}) collective-permute-start(bf16[48,2176]{1,0:T(8,128)(2,1)S(1)} %get-tuple-element.90), channel_id=1, source_target_pairs={{0,2},{1,3},{2,0},{3,1},{4,6},{5,7},{6,4},{7,5},{8,10},{9,11},{10,... | collective-permute-start | bytes 626696 | tf_op jit(solution)/shard_map/ppermute | solution.py:23
  203.8 30.3 %collective-permute-start.31 = (bf16[64,2048]{1,0:T(8,128)(2,1)S(1)}, bf16[64,2048]{1,0:T(8,128)(2,1)S(1)}, u32[]{:S(2)}, u32[]{:S(2)}) collective-permute-start(bf16[64,2048]{1,0:T(8,128)(2,1)S(1)} %pad_maximum_fusion.19), channel_id=1, source_target_pairs={{0,24},{1,25},{2,26},{3,27},{4,28},{5,29},{6,30},{7,31},{8,16},{9,... | collective-permute-start | bytes 786440 | tf_op jit(solution)/shard_map/ppermute | solution.py:84
  215.9 18.2 %collective-permute-start.30 = (bf16[64,2048]{1,0:T(8,128)(2,1)S(1)}, bf16[64,2048]{1,0:T(8,128)(2,1)S(1)}, u32[]{:S(2)}, u32[]{:S(2)}) collective-permute-start(bf16[64,2048]{1,0:T(8,128)(2,1)S(1)} %pad_maximum_fusion.18), channel_id=1, source_target_pairs={{0,16},{1,17},{2,18},{3,19},{4,20},{5,21},{6,22},{7,23},{8,24},{9,... | collective-permute-start | bytes 786440 | tf_op jit(solution)/shard_map/ppermute | solution.py:85
  216.1 22.4 %collective-permute-start.42 = (bf16[64,2176]{1,0:T(8,128)(2,1)S(1)}, bf16[64,2176]{1,0:T(8,128)(2,1)S(1)}, u32[]{:S(2)}, u32[]{:S(2)}) collective-permute-start(bf16[64,2176]{1,0:T(8,128)(2,1)S(1)} %pad_maximum_fusion.16), channel_id=1, source_target_pairs={{0,24},{1,25},{2,26},{3,27},{4,28},{5,29},{6,30},{7,31},{8,16},{9,... | collective-permute-start | bytes 835592 | tf_op jit(solution)/shard_map/ppermute | solution.py:84
  220.0 18.6 %collective-permute-start.41 = (bf16[64,2176]{1,0:T(8,128)(2,1)S(1)}, bf16[64,2176]{1,0:T(8,128)(2,1)S(1)}, u32[]{:S(2)}, u32[]{:S(2)}) collective-permute-start(bf16[64,2176]{1,0:T(8,128)(2,1)S(1)} %pad_maximum_fusion.15), channel_id=1, source_target_pairs={{0,16},{1,17},{2,18},{3,19},{4,20},{5,21},{6,22},{7,23},{8,24},{9,... | collective-permute-start | bytes 835592 | tf_op jit(solution)/shard_map/ppermute | solution.py:85

commit v2 on v1

--- a/solution.py
+++ b/solution.py
@@ -54,7 +54,8 @@
 def spread_rest(kept, size, parts):
     for step in range(len(parts[0][2]) - 1):
         got = send_all(kept, size, parts, step)
-        kept = [jnp.concatenate([k, g]) for k, g in zip(kept, got)]
+        for k in range(len(kept)):
+            kept[k] = jnp.concatenate([kept[k], got[k]])
     return kept, send_all(kept, size, parts, -1)
 
 
@@ -496,7 +497,7 @@
     dx_kept, dh_kept, wa_kept = back_rows(places, xd_kept, xf_kept, w_gu, w_dn, groups)
     xd_new = after(xd_new, dx_kept)
     if groups == 1:
-        y_new = after(y_new, xd_new)
+        y_new = [y_new[0], *after(y_new[1:], xd_new)]
     dx_new, dh_new, wa_new = back_rows(places, xd_new, xf_new, w_gu, w_dn, groups)
     if groups == 1:
         comb_rows = forward_first(y_kept, y_new, dx_new)

time: 240 us -> 240 us (level)
    ppermute x39, waiting for transfers between devices: 59 us -> 62.8 us  [send(): lax.ppermute(array, 'expert', [(i, i ^ 1 << bit) for i in range(size)])]
    ppermute x39, starting transfers between devices: 46.7 us -> 43 us  [send(): lax.ppermute(array, 'expert', [(i, i ^ 1 << bit) for i in range(size)])]
where the time goes in v2:
time: 240 us
  waiting for transfers between devices  78.4 us (33%)
  Pallas kernels  72.3 us (30%)
  starting transfers between devices  68.3 us (28%)
  other arithmetic  15.2 us (6%)
  local copies, waits for them, and re-layouts  4.23 us (2%)
    ppermute x39, waiting for transfers between devices, send(): lax.ppermute(array, 'expert', [(i, i ^ 1 << bit) for i in range(size)])  62.8 us
    ppermute x39, starting transfers between devices, send(): lax.ppermute(array, 'expert', [(i, i ^ 1 << bit) for i in range(size)])  43 us
    pallas_call x2, Pallas kernels, back_rows(): pl.pallas_call(lambda *refs: back_kernel(counts, groups, *refs), grid_spe...  31.6 us
    pallas_call x2, Pallas kernels, forward_rows(): pl.pallas_call(lambda *refs: forward_kernel(counts, groups, *refs), grid_...  22.4 us
    pallas_call x2, Pallas kernels, weight_grad(): pl.pallas_call(lambda *refs: weight_kernel(left_counts, right_counts, lef...  18.3 us
    ppermute x2, starting transfers between devices, collect_rest(): other = lax.ppermute(other, ('segment', 'expert'), cross(size // 2))  17.6 us
    ppermute x2, waiting for transfers between devices, collect_rest(): other = lax.ppermute(other, ('segment', 'expert'), cross(size // 2))  15.7 us
    ppermute x1, starting transfers between devices, shards(): other_routes = lax.ppermute(bwd_routes[0], 'segment', swap)  7.57 us
  transfers between devices with their start and end apart: 44, of which 17 were waited for; matrix products, arithmetic and copies ran while one was open for 7% of the time, Pallas kernels for 30%

profile of v2, /device:TPU:1, one launch (start us, length us, event | category | flops | bytes accessed | tf_op | source)
XLA Modules:
  0.0 239.8 jit_solution(17524090969019913517)
XLA Ops:
  0.6 3.2 %collective-permute-start = (bf16[64,2048]{1,0:T(8,128)(2,1)}, bf16[64,2048]{1,0:T(8,128)(2,1)S(1)}, u32[]{:S(2)}, u32[]{:S(2)}) collective-permute-start(bf16[64,2048]{1,0:T(8,128)(2,1)} %bitcast.25), channel_id=1, source_target_pairs={{0,8},{1,9},{2,10},{3,11},{4,12},{5,13},{6,14},{7,15},{8,0},{9,1},... | collective-permute-start | bytes 786440 | tf_op jit(solution)/shard_map/ppermute | solution.py:23
  4.5 0.7 select_reduce_fusion.1
  6.0 0.7 select_reduce_fusion.2
  6.9 1.0 pad_maximum_fusion.23
  8.0 1.1 pad_maximum_fusion.8
  9.1 7.0 %collective-permute-done = bf16[64,2048]{1,0:T(8,128)(2,1)S(1)} collective-permute-done((bf16[64,2048]{1,0:T(8,128)(2,1)}, bf16[64,2048]{1,0:T(8,128)(2,1)S(1)}, u32[]{:S(2)}, u32[]{:S(2)}) %collective-permute-start) | collective-permute-done | bytes 262176 | tf_op jit(solution)/shard_map/ppermute | solution.py:23
  16.6 1.1 collective-permute-start.2
  17.7 1.3 collective-permute-start.4
  19.0 4.6 %collective-permute-start.6 = (bf16[48,2176]{1,0:T(8,128)(2,1)S(1)}, bf16[48,2176]{1,0:T(8,128)(2,1)S(1)}, u32[]{:S(2)}, u32[]{:S(2)}) collective-permute-start(bf16[48,2176]{1,0:T(8,128)(2,1)S(1)} %pad_maximum_fusion.21), channel_id=1, source_target_pairs={{0,4},{1,5},{2,6},{3,7},{4,0},{5,1},{6,2},{7,3},{8,12},{9,13},{10,... | collective-permute-start | bytes 626696 | tf_op jit(solution)/shard_map/ppermute | solution.py:23
  23.9 4.1 %collective-permute-start.5 = (bf16[96,2176]{1,0:T(8,128)(2,1)S(1)}, bf16[96,2176]{1,0:T(8,128)(2,1)S(1)}, u32[]{:S(2)}, u32[]{:S(2)}) collective-permute-start(bf16[96,2176]{1,0:T(8,128)(2,1)S(1)} %pad_maximum_fusion.10), channel_id=1, source_target_pairs={{0,4},{1,5},{2,6},{3,7},{4,0},{5,1},{6,2},{7,3},{8,12},{9,13},{10,... | collective-permute-start | bytes 1253384 | tf_op jit(solution)/shard_map/ppermute | solution.py:23
  28.0 3.3 %collective-permute-done.6 = bf16[48,2176]{1,0:T(8,128)(2,1)S(1)} collective-permute-done((bf16[48,2176]{1,0:T(8,128)(2,1)S(1)}, bf16[48,2176]{1,0:T(8,128)(2,1)S(1)}, u32[]{:S(2)}, u32[]{:S(2)}) %collective-permute-start.6) | collective-permute-done | bytes 208928 | tf_op jit(solution)/shard_map/ppermute | solution.py:23
  31.4 0.8 collective-permute-start.7
  32.2 2.3 collective-permute-start.8
  34.5 6.4 %collective-permute-done.12 = bf16[64,4096]{1,0:T(8,128)(2,1)S(1)} collective-permute-done((bf16[64,4096]{1,0:T(8,128)(2,1)S(1)}, bf16[64,4096]{1,0:T(8,128)(2,1)S(1)}, u32[]{:S(2)}, u32[]{:S(2)}) %collective-permute-start.12) | collective-permute-done | bytes 524320 | tf_op jit(solution)/shard_map/ppermute | solution.py:23
  41.0 0.8 collective-permute-start.13
  41.8 1.3 collective-permute-start.16
  43.2 1.3 collective-permute-done.5
  44.5 1.0 collective-permute-start.9
  45.6 1.0 pad_maximum_fusion.4.refs_3_.refs_6_
  46.5 10.9 %shard_map.128 = (bf16[128,2048]{1,0:T(8,128)(2,1)S(1)}, bf16[192,2048]{1,0:T(8,128)(2,1)S(1)}, bf16[192,2048]{1,0:T(8,128)(2,1)S(1)}) custom-call(s32[2]{0:T(128)S(1)} %pad_add_fusion.refs_0_, bf16[128,2176]{1,0:T(8,128)(2,1)S(1)} %pad_maximum_fusion.7.refs_1_.refs_4_, bf16[192,2176]{1,0:T(8,128)(2,1)S(1)} %pad_maximum_fusion.3.refs_2_.refs_5_, ...), custom_call_target="tpu_custom_call" | custom-call | flops 4831838208 | bytes 13631488 | tf_op jit(solution)/shard_map/pallas_call | solution.py:336
  57.5 1.3 collective-permute-start.10
  58.8 6.0 %collective-permute-done.19 = bf16[48,4096]{1,0:T(8,128)(2,1)S(1)} collective-permute-done((bf16[48,4096]{1,0:T(8,128)(2,1)S(1)}, bf16[48,4096]{1,0:T(8,128)(2,1)S(1)}, u32[]{:S(2)}, u32[]{:S(2)}) %collective-permute-start.19) | collective-permute-done | bytes 393248 | tf_op jit(solution)/shard_map/ppermute | solution.py:23
  64.9 1.0 collective-permute-start.20
  66.0 14.9 %collective-permute-done.17 = bf16[96,4096]{1,0:T(8,128)(2,1)S(1)} collective-permute-done((bf16[96,4096]{1,0:T(8,128)(2,1)S(1)}, bf16[96,4096]{1,0:T(8,128)(2,1)S(1)}, u32[]{:S(2)}, u32[]{:S(2)}) %collective-permute-start.17) | collective-permute-done | bytes 786464 | tf_op jit(solution)/shard_map/ppermute | solution.py:23
  80.8 1.0 collective-permute-start.14
  81.9 1.6 collective-permute-start.18
  83.5 1.3 pad_maximum_fusion.1.refs_3_.refs_2_.refs_4_
  84.8 5.0 %collective-permute-done.14 = bf16[64,4096]{1,0:T(8,128)(2,1)S(1)} collective-permute-done((bf16[64,4096]{1,0:T(8,128)(2,1)S(1)}, bf16[64,4096]{1,0:T(8,128)(2,1)S(1)}, u32[]{:S(2)}, u32[]{:S(2)}) %collective-permute-start.14) | collective-permute-done | bytes 524320 | tf_op jit(solution)/shard_map/ppermute | solution.py:23
  89.8 1.1 collective-permute-start.21
  91.0 7.6 %collective-permute-start.43 = (s32[64,8]{0,1:T(8,128)S(1)}, s32[64,8]{0,1:T(8,128)S(1)}, u32[]{:S(2)}, u32[]{:S(2)}) collective-permute-start(s32[64,8]{0,1:T(8,128)S(1)} %bitcast.32), channel_id=1, source_target_pairs={{0,16},{16,0},{1,17},{17,1},{2,18},{18,2},{3,19},{19,3},{4,20},{20... | collective-permute-start | bytes 6152 | tf_op jit(solution)/shard_map/ppermute | solution.py:492
  98.6 0.9 copy-done.13
  99.5 11.5 %shard_map.129 = (bf16[128,2048]{1,0:T(8,128)(2,1)}, bf16[192,2048]{1,0:T(8,128)(2,1)}, bf16[192,2048]{1,0:T(8,128)(2,1)}) custom-call(s32[2]{0:T(128)S(1)} %pad_add_fusion.refs_0_, bf16[128,2176]{1,0:T(8,128)(2,1)S(1)} %collective-permute-done.8.refs_1_.refs_4_, bf16[192,2176]{1,0:T(8,128)(2,1)S(1)} %collective-permute-done.9.refs_2_.refs_5_, ...), custom_call_target="tpu_custom_call" | custom-call | flops 4831838208 | bytes 13631488 | tf_op jit(solution)/shard_map/pallas_call | solution.py:336
  111.0 1.5 collective-permute-start.11
  112.5 15.8 %shard_map.130 = (bf16[128,2176]{1,0:T(8,128)(2,1)S(1)}, bf16[192,2176]{1,0:T(8,128)(2,1)S(1)}, bf16[192,2176]{1,0:T(8,128)(2,1)S(1)}, bf16[512,1536]{1,0:T(8,128)(2,1)}, bf16[512,768]{1,0:T(8,128)(2,1)S(1)}) custom-call(s32[2]{0:T(128)S(1)} %pad_add_fusion.refs_0_, bf16[128,4096]{1,0:T(8,128)(2,1)} %copy-done.2, bf16[192,4096]{1,0:T(8,128)(2,1)} %copy-done, ...), custom_call_target="tpu_custom_call" | custom-call | flops 8053063680 | bytes 18350080 | tf_op jit(solution)/shard_map/pallas_call | solution.py:243
  129.3 15.8 %shard_map.131 = (bf16[128,2176]{1,0:T(8,128)(2,1)S(1)}, bf16[192,2176]{1,0:T(8,128)(2,1)S(1)}, bf16[192,2176]{1,0:T(8,128)(2,1)S(1)}, bf16[512,1536]{1,0:T(8,128)(2,1)}, bf16[512,768]{1,0:T(8,128)(2,1)S(1)}) custom-call(s32[2]{0:T(128)S(1)} %pad_add_fusion.refs_0_, bf16[128,4096]{1,0:T(8,128)(2,1)} %copy-done.4, ...), custom_call_target="tpu_custom_call" | custom-call | flops 8053063680 | bytes 18350080 | tf_op jit(solution)/shard_map/pallas_call | solution.py:243
  145.3 1.2 copy-done.5
  146.5 11.4 %shard_map.132 = bf16[2048,1536]{1,0:T(8,128)(2,1)} custom-call(bf16[128,4096]{1,0:T(8,128)(2,1)S(1)} %copy-done.3, bf16[192,4096]{1,0:T(8,128)(2,1)S(1)} %copy-done.1, bf16[192,4096]{1,0:T(8,128)(2,1)} %pad_maximum_fusion.1.refs_3_.refs_2_.refs_4_, bf16[128,4096]{1,0:T(8,128)(2,1)S(1)} %copy-done.5, ...), custom_call_target="tpu_custom_call" | custom-call | flops 6442450944 | bytes 13631488 | tf_op jit(solution)/shard_map/pallas_call | solution.py:421
  158.0 1.2 collective-permute-start.33
  159.2 0.9 copy-done.10
  160.0 0.9 collective-permute-start.34
  160.9 2.1 add_convert_fusion.5
  164.0 1.2 add_convert_fusion.12
  165.1 6.8 %shard_map.133 = bf16[768,2048]{1,0:T(8,128)(2,1)} custom-call(bf16[512,768]{1,0:T(8,128)(2,1)S(1)} %get-tuple-element.73.refs_0_, bf16[512,768]{1,0:T(8,128)(2,1)S(1)} %get-tuple-element.74.refs_1_, bf16[128,4096]{1,0:T(8,128)(2,1)S(1)} %copy-done.3, bf16[192,4096]{1,0:T(8,128)(2,1)} %copy-done, ...), custom_call_target="tpu_custom_call" | custom-call | flops 3221225472 | bytes 8912896 | tf_op jit(solution)/shard_map/pallas_call | solution.py:421
  172.0 1.5 collective-permute-start.26
  173.5 1.7 collective-permute-done.33
  175.2 2.0 collective-permute-start.24
  177.2 0.9 collective-permute-done.34
  178.2 0.8 collective-permute-start.39
  179.3 4.2 %collective-permute-done.24 = bf16[64,2048]{1,0:T(8,128)(2,1)S(1)} collective-permute-done((bf16[64,2048]{1,0:T(8,128)(2,1)S(1)}, bf16[64,2048]{1,0:T(8,128)(2,1)S(1)}, u32[]{:S(2)}, u32[]{:S(2)}) %collective-permute-start.24) | collective-permute-done | bytes 262176 | tf_op jit(solution)/shard_map/ppermute | solution.py:23
  183.6 0.9 collective-permute-start.35
  184.5 7.2 %collective-permute-done.35 = bf16[64,2176]{1,0:T(8,128)(2,1)S(1)} collective-permute-done((bf16[64,2176]{1,0:T(8,128)(2,1)S(1)}, bf16[64,2176]{1,0:T(8,128)(2,1)S(1)}, u32[]{:S(2)}, u32[]{:S(2)}) %collective-permute-start.35) | collective-permute-done | bytes 278560 | tf_op jit(solution)/shard_map/ppermute | solution.py:23
  191.7 1.1 collective-permute-start.37
  193.0 1.1 add_convert_fusion.18
  194.1 1.5 collective-permute-start.36
  195.7 1.7 collective-permute-done.25
  197.4 1.4 collective-permute-start.29
  199.2 1.0 collective-permute-start.40
  200.9 2.4 collective-permute-done.29
  203.8 12.4 %collective-permute-start.31 = (bf16[64,2048]{1,0:T(8,128)(2,1)S(1)}, bf16[64,2048]{1,0:T(8,128)(2,1)S(1)}, u32[]{:S(2)}, u32[]{:S(2)}) collective-permute-start(bf16[64,2048]{1,0:T(8,128)(2,1)S(1)} %pad_maximum_fusion.19), channel_id=1, source_target_pairs={{0,24},{1,25},{2,26},{3,27},{4,28},{5,29},{6,30},{7,31},{8,16},{9,... | collective-permute-start | bytes 786440 | tf_op jit(solution)/shard_map/ppermute | solution.py:85
  216.5 5.3 %collective-permute-start.42 = (bf16[64,2176]{1,0:T(8,128)(2,1)S(1)}, bf16[64,2176]{1,0:T(8,128)(2,1)S(1)}, u32[]{:S(2)}, u32[]{:S(2)}) collective-permute-start(bf16[64,2176]{1,0:T(8,128)(2,1)S(1)} %pad_maximum_fusion.16), channel_id=1, source_target_pairs={{0,24},{1,25},{2,26},{3,27},{4,28},{5,29},{6,30},{7,31},{8,16},{9,... | collective-permute-start | bytes 835592 | tf_op jit(solution)/shard_map/ppermute | solution.py:85
  221.8 12.3 %collective-permute-done.31 = bf16[64,2048]{1,0:T(8,128)(2,1)S(1)} collective-permute-done((bf16[64,2048]{1,0:T(8,128)(2,1)S(1)}, bf16[64,2048]{1,0:T(8,128)(2,1)S(1)}, u32[]{:S(2)}, u32[]{:S(2)}) %collective-permute-start.31) | collective-permute-done | bytes 262176 | tf_op jit(solution)/shard_map/ppermute | solution.py:85
  234.1 0.8 fusion
  234.9 3.4 %collective-permute-done.42 = bf16[64,2176]{1,0:T(8,128)(2,1)S(1)} collective-permute-done((bf16[64,2176]{1,0:T(8,128)(2,1)S(1)}, bf16[64,2176]{1,0:T(8,128)(2,1)S(1)}, u32[]{:S(2)}, u32[]{:S(2)}) %collective-permute-start.42) | collective-permute-done | bytes 278560 | tf_op jit(solution)/shard_map/ppermute | solution.py:85
  238.3 0.7 fusion.1
  (123 shorter events, 8.8 us)
Async XLA Ops:
  0.6 8.4 %copy-start.8 = (bf16[1,64,2048]{2,1,0:T(8,128)(2,1)S(1)}, bf16[1,64,2048]{2,1,0:T(8,128)(2,1)}, u32[]{:S(2)}) copy-start(bf16[1,64,2048]{2,1,0:T(8,128)(2,1)} %param.9) | copy-start | bytes 786436
  0.6 15.4 %collective-permute-start = (bf16[64,2048]{1,0:T(8,128)(2,1)}, bf16[64,2048]{1,0:T(8,128)(2,1)S(1)}, u32[]{:S(2)}, u32[]{:S(2)}) collective-permute-start(bf16[64,2048]{1,0:T(8,128)(2,1)} %bitcast.25), channel_id=1, source_target_pairs={{0,8},{1,9},{2,10},{3,11},{4,12},{5,13},{6,14},{7,15},{8,0},{9,1},... | collective-permute-start | bytes 786440 | tf_op jit(solution)/shard_map/ppermute | solution.py:23
  6.9 9.5 %collective-permute-start.1 = (bf16[64,128]{1,0:T(8,128)(2,1)S(1)}, bf16[64,128]{1,0:T(8,128)(2,1)S(1)}, u32[]{:S(2)}, u32[]{:S(2)}) collective-permute-start(bf16[64,128]{1,0:T(8,128)(2,1)S(1)} %fusion.4), channel_id=1, source_target_pairs={{0,8},{1,9},{2,10},{3,11},{4,12},{5,13},{6,14},{7,15},{8,0},{9,1},... | collective-permute-start | bytes 49160 | tf_op jit(solution)/shard_map/ppermute | solution.py:23
  16.4 24.5 %collective-permute-start.12 = (bf16[64,4096]{1,0:T(8,128)(2,1)S(1)}, bf16[64,4096]{1,0:T(8,128)(2,1)S(1)}, u32[]{:S(2)}, u32[]{:S(2)}) collective-permute-start(bf16[64,4096]{1,0:T(8,128)(2,1)S(1)} %pad_maximum_fusion.8), channel_id=1, source_target_pairs={{0,8},{1,9},{2,10},{3,11},{4,12},{5,13},{6,14},{7,15},{8,0},{9,1},... | collective-permute-start | bytes 1572872 | tf_op jit(solution)/shard_map/ppermute | solution.py:23
  16.6 7.0 %collective-permute-start.2 = (bf16[32,2176]{1,0:T(8,128)(2,1)S(1)}, bf16[32,2176]{1,0:T(8,128)(2,1)S(1)}, u32[]{:S(2)}, u32[]{:S(2)}) collective-permute-start(bf16[32,2176]{1,0:T(8,128)(2,1)S(1)} %pad_maximum_fusion.22), channel_id=1, source_target_pairs={{0,1},{1,0},{2,3},{3,2},{4,5},{5,4},{6,7},{7,6},{8,9},{9,8},{10,11... | collective-permute-start | bytes 417800 | tf_op jit(solution)/shard_map/ppermute | solution.py:23
  17.7 6.2 %collective-permute-start.4 = (bf16[48,2176]{1,0:T(8,128)(2,1)S(1)}, bf16[48,2176]{1,0:T(8,128)(2,1)S(1)}, u32[]{:S(2)}, u32[]{:S(2)}) collective-permute-start(bf16[48,2176]{1,0:T(8,128)(2,1)S(1)} %pad_maximum_fusion.20), channel_id=1, source_target_pairs={{0,2},{1,3},{2,0},{3,1},{4,6},{5,7},{6,4},{7,5},{8,10},{9,11},{10,... | collective-permute-start | bytes 626696 | tf_op jit(solution)/shard_map/ppermute | solution.py:23
  19.0 12.3 %collective-permute-start.6 = (bf16[48,2176]{1,0:T(8,128)(2,1)S(1)}, bf16[48,2176]{1,0:T(8,128)(2,1)S(1)}, u32[]{:S(2)}, u32[]{:S(2)}) collective-permute-start(bf16[48,2176]{1,0:T(8,128)(2,1)S(1)} %pad_maximum_fusion.21), channel_id=1, source_target_pairs={{0,4},{1,5},{2,6},{3,7},{4,0},{5,1},{6,2},{7,3},{8,12},{9,13},{10,... | collective-permute-start | bytes 626696 | tf_op jit(solution)/shard_map/ppermute | solution.py:23
  23.6 8.6 %collective-permute-start.3 = (bf16[64,2176]{1,0:T(8,128)(2,1)S(1)}, bf16[64,2176]{1,0:T(8,128)(2,1)S(1)}, u32[]{:S(2)}, u32[]{:S(2)}) collective-permute-start(bf16[64,2176]{1,0:T(8,128)(2,1)S(1)} %pad_maximum_fusion.14), channel_id=1, source_target_pairs={{0,2},{1,3},{2,0},{3,1},{4,6},{5,7},{6,4},{7,5},{8,10},{9,11},{10,... | collective-permute-start | bytes 835592 | tf_op jit(solution)/shard_map/ppermute | solution.py:23
  23.9 20.5 %collective-permute-start.5 = (bf16[96,2176]{1,0:T(8,128)(2,1)S(1)}, bf16[96,2176]{1,0:T(8,128)(2,1)S(1)}, u32[]{:S(2)}, u32[]{:S(2)}) collective-permute-start(bf16[96,2176]{1,0:T(8,128)(2,1)S(1)} %pad_maximum_fusion.10), channel_id=1, source_target_pairs={{0,4},{1,5},{2,6},{3,7},{4,0},{5,1},{6,2},{7,3},{8,12},{9,13},{10,... | collective-permute-start | bytes 1253384 | tf_op jit(solution)/shard_map/ppermute | solution.py:23
  31.4 13.2 %collective-permute-start.7 = (bf16[96,2176]{1,0:T(8,128)(2,1)S(1)}, bf16[96,2176]{1,0:T(8,128)(2,1)S(1)}, u32[]{:S(2)}, u32[]{:S(2)}) collective-permute-start(bf16[96,2176]{1,0:T(8,128)(2,1)S(1)} %pad_maximum_fusion.11), channel_id=1, source_target_pairs={{0,1},{1,0},{2,3},{3,2},{4,5},{5,4},{6,7},{7,6},{8,9},{9,8},{10,11... | collective-permute-start | bytes 1253384 | tf_op jit(solution)/shard_map/ppermute | solution.py:23
  32.2 58.7 %collective-permute-start.8 = (bf16[128,2176]{1,0:T(8,128)(2,1)S(1)}, bf16[128,2176]{1,0:T(8,128)(2,1)S(1)}, u32[]{:S(2)}, u32[]{:S(2)}) collective-permute-start(bf16[128,2176]{1,0:T(8,128)(2,1)S(1)} %pad_maximum_fusion.7.refs_1_.refs_4_), channel_id=1, source_target_pairs={{0,4},{1,5},{2,6},{3,7},{4,0},{5,1},{6,2},{7,3},{8,12},{9,13},{10,... | collective-permute-start | bytes 1671176 | tf_op jit(solution)/shard_map/ppermute | solution.py:23
  41.0 23.9 %collective-permute-start.13 = (bf16[32,4096]{1,0:T(8,128)(2,1)S(1)}, bf16[32,4096]{1,0:T(8,128)(2,1)S(1)}, u32[]{:S(2)}, u32[]{:S(2)}) collective-permute-start(bf16[32,4096]{1,0:T(8,128)(2,1)S(1)} %pad_maximum_fusion.17), channel_id=1, source_target_pairs={{0,1},{1,0},{2,3},{3,2},{4,5},{5,4},{6,7},{7,6},{8,9},{9,8},{10,11... | collective-permute-start | bytes 786440 | tf_op jit(solution)/shard_map/ppermute | solution.py:23
  41.8 15.6 %collective-permute-start.16 = (bf16[48,4096]{1,0:T(8,128)(2,1)S(1)}, bf16[48,4096]{1,0:T(8,128)(2,1)S(1)}, u32[]{:S(2)}, u32[]{:S(2)}) collective-permute-start(bf16[48,4096]{1,0:T(8,128)(2,1)S(1)} %pad_maximum_fusion.12), channel_id=1, source_target_pairs={{0,2},{1,3},{2,0},{3,1},{4,6},{5,7},{6,4},{7,5},{8,10},{9,11},{10,... | collective-permute-start | bytes 1179656 | tf_op jit(solution)/shard_map/ppermute | solution.py:23
  44.5 20.4 %collective-permute-start.19 = (bf16[48,4096]{1,0:T(8,128)(2,1)S(1)}, bf16[48,4096]{1,0:T(8,128)(2,1)S(1)}, u32[]{:S(2)}, u32[]{:S(2)}) collective-permute-start(bf16[48,4096]{1,0:T(8,128)(2,1)S(1)} %pad_maximum_fusion.13), channel_id=1, source_target_pairs={{0,4},{1,5},{2,6},{3,7},{4,0},{5,1},{6,2},{7,3},{8,12},{9,13},{10,... | collective-permute-start | bytes 1179656 | tf_op jit(solution)/shard_map/ppermute | solution.py:23
  44.5 12.9 %copy-start.6 = (bf16[192,2176]{1,0:T(8,128)(2,1)}, bf16[192,2176]{1,0:T(8,128)(2,1)S(1)}, u32[]{:S(2)}) copy-start(bf16[192,2176]{1,0:T(8,128)(2,1)S(1)} %pad_maximum_fusion.3.refs_2_.refs_5_) | copy-start | bytes 2506756
  44.5 54.0 %collective-permute-start.9 = (bf16[192,2176]{1,0:T(8,128)(2,1)S(1)}, bf16[192,2176]{1,0:T(8,128)(2,1)S(1)}, u32[]{:S(2)}, u32[]{:S(2)}) collective-permute-start(bf16[192,2176]{1,0:T(8,128)(2,1)S(1)} %pad_maximum_fusion.3.refs_2_.refs_5_), channel_id=1, source_target_pairs={{0,1},{1,0},{2,3},{3,2},{4,5},{5,4},{6,7},{7,6},{8,9},{9,8},{10,11... | collective-permute-start | bytes 2506760 | tf_op jit(solution)/shard_map/ppermute | solution.py:23
  46.5 10.9 %copy-start.9 = (bf16[192,2176]{1,0:T(8,128)(2,1)S(1)}, bf16[192,2176]{1,0:T(8,128)(2,1)}, u32[]{:S(2)}) copy-start(bf16[192,2176]{1,0:T(8,128)(2,1)} %pad_maximum_fusion.4.refs_3_.refs_6_) | copy-start | bytes 2506756
  57.5 41.1 %collective-permute-start.10 = (bf16[192,2176]{1,0:T(8,128)(2,1)S(1)}, bf16[192,2176]{1,0:T(8,128)(2,1)S(1)}, u32[]{:S(2)}, u32[]{:S(2)}) collective-permute-start(bf16[192,2176]{1,0:T(8,128)(2,1)S(1)} %copy-done.9), channel_id=1, source_target_pairs={{0,2},{1,3},{2,0},{3,1},{4,6},{5,7},{6,4},{7,5},{8,10},{9,11},{10,... | collective-permute-start | bytes 2506760 | tf_op jit(solution)/shard_map/ppermute | solution.py:23
  64.8 16.0 %collective-permute-start.17 = (bf16[96,4096]{1,0:T(8,128)(2,1)S(1)}, bf16[96,4096]{1,0:T(8,128)(2,1)S(1)}, u32[]{:S(2)}, u32[]{:S(2)}) collective-permute-start(bf16[96,4096]{1,0:T(8,128)(2,1)S(1)} %pad_maximum_fusion.5), channel_id=1, source_target_pairs={{0,4},{1,5},{2,6},{3,7},{4,0},{5,1},{6,2},{7,3},{8,12},{9,13},{10,... | collective-permute-start | bytes 2359304 | tf_op jit(solution)/shard_map/ppermute | solution.py:23
  64.9 17.0 %collective-permute-start.20 = (bf16[96,4096]{1,0:T(8,128)(2,1)S(1)}, bf16[96,4096]{1,0:T(8,128)(2,1)S(1)}, u32[]{:S(2)}, u32[]{:S(2)}) collective-permute-start(bf16[96,4096]{1,0:T(8,128)(2,1)S(1)} %pad_maximum_fusion.6), channel_id=1, source_target_pairs={{0,1},{1,0},{2,3},{3,2},{4,5},{5,4},{6,7},{7,6},{8,9},{9,8},{10,11... | collective-permute-start | bytes 2359304 | tf_op jit(solution)/shard_map/ppermute | solution.py:23
  80.8 9.0 %collective-permute-start.14 = (bf16[64,4096]{1,0:T(8,128)(2,1)S(1)}, bf16[64,4096]{1,0:T(8,128)(2,1)S(1)}, u32[]{:S(2)}, u32[]{:S(2)}) collective-permute-start(bf16[64,4096]{1,0:T(8,128)(2,1)S(1)} %pad_maximum_fusion.9), channel_id=1, source_target_pairs={{0,2},{1,3},{2,0},{3,1},{4,6},{5,7},{6,4},{7,5},{8,10},{9,11},{10,... | collective-permute-start | bytes 1572872 | tf_op jit(solution)/shard_map/ppermute | solution.py:23
  81.9 9.0 %copy-start = (bf16[192,4096]{1,0:T(8,128)(2,1)}, bf16[192,4096]{1,0:T(8,128)(2,1)S(1)}, u32[]{:S(2)}) copy-start(bf16[192,4096]{1,0:T(8,128)(2,1)S(1)} %pad_maximum_fusion.refs_2_.refs_1_.refs_3_) | copy-start | bytes 4718596
  81.9 46.4 %collective-permute-start.18 = (bf16[192,4096]{1,0:T(8,128)(2,1)S(1)}, bf16[192,4096]{1,0:T(8,128)(2,1)}, u32[]{:S(2)}, u32[]{:S(2)}) collective-permute-start(bf16[192,4096]{1,0:T(8,128)(2,1)S(1)} %pad_maximum_fusion.refs_2_.refs_1_.refs_3_), channel_id=1, source_target_pairs={{0,1},{1,0},{2,3},{3,2},{4,5},{5,4},{6,7},{7,6},{8,9},{9,8},{10,11... | collective-permute-start | bytes 4718600 | tf_op jit(solution)/shard_map/ppermute | solution.py:23
  84.8 6.2 %copy-start.12 = (s32[1,64,8]{1,2,0:T(8,128)S(1)}, s32[1,64,8]{1,2,0:T(8,128)}, u32[]{:S(2)}) copy-start(s32[1,64,8]{1,2,0:T(8,128)} %param.13) | copy-start | bytes 6148
  89.8 38.6 %collective-permute-start.21 = (bf16[192,4096]{1,0:T(8,128)(2,1)}, bf16[192,4096]{1,0:T(8,128)(2,1)}, u32[]{:S(2)}, u32[]{:S(2)}) collective-permute-start(bf16[192,4096]{1,0:T(8,128)(2,1)} %pad_maximum_fusion.1.refs_3_.refs_2_.refs_4_), channel_id=1, source_target_pairs={{0,2},{1,3},{2,0},{3,1},{4,6},{5,7},{6,4},{7,5},{8,10},{9,11},{10,... | collective-permute-start | bytes 4718600 | tf_op jit(solution)/shard_map/ppermute | solution.py:23
  90.9 20.0 %copy-start.2 = (bf16[128,4096]{1,0:T(8,128)(2,1)}, bf16[128,4096]{1,0:T(8,128)(2,1)S(1)}, u32[]{:S(2)}) copy-start(bf16[128,4096]{1,0:T(8,128)(2,1)S(1)} %pad_maximum_fusion.2.refs_1_.refs_0_.refs_2_) | copy-start | bytes 3145732
  91.0 148.2 %collective-permute-start.43 = (s32[64,8]{0,1:T(8,128)S(1)}, s32[64,8]{0,1:T(8,128)S(1)}, u32[]{:S(2)}, u32[]{:S(2)}) collective-permute-start(s32[64,8]{0,1:T(8,128)S(1)} %bitcast.32), channel_id=1, source_target_pairs={{0,16},{16,0},{1,17},{17,1},{2,18},{18,2},{3,19},{19,3},{4,20},{20... | collective-permute-start | bytes 6152 | tf_op jit(solution)/shard_map/ppermute | solution.py:492
  98.6 12.5 %copy-start.7 = (bf16[192,2176]{1,0:T(8,128)(2,1)}, bf16[192,2176]{1,0:T(8,128)(2,1)S(1)}, u32[]{:S(2)}) copy-start(bf16[192,2176]{1,0:T(8,128)(2,1)S(1)} %collective-permute-done.9.refs_2_.refs_5_) | copy-start | bytes 2506756
  98.6 29.8 %collective-permute-start.15 = (bf16[128,4096]{1,0:T(8,128)(2,1)S(1)}, bf16[128,4096]{1,0:T(8,128)(2,1)S(1)}, u32[]{:S(2)}, u32[]{:S(2)}) collective-permute-start(bf16[128,4096]{1,0:T(8,128)(2,1)S(1)} %pad_maximum_fusion.2.refs_1_.refs_0_.refs_2_), channel_id=1, source_target_pairs={{0,4},{1,5},{2,6},{3,7},{4,0},{5,1},{6,2},{7,3},{8,12},{9,13},{10,... | collective-permute-start | bytes 3145736 | tf_op jit(solution)/shard_map/ppermute | solution.py:23
  98.6 1.0 copy-start.13
  111.0 46.9 %collective-permute-start.11 = (bf16[128,2048]{1,0:T(8,128)(2,1)}, bf16[128,2048]{1,0:T(8,128)(2,1)}, u32[]{:S(2)}, u32[]{:S(2)}) collective-permute-start(bf16[128,2048]{1,0:T(8,128)(2,1)} %get-tuple-element.46), channel_id=1, source_target_pairs={{0,4},{1,5},{2,6},{3,7},{4,0},{5,1},{6,2},{7,3},{8,12},{9,13},{10,... | collective-permute-start | bytes 1572872 | tf_op jit(solution)/shard_map/ppermute | solution.py:23
  128.3 1.0 copy-start.4
  128.4 16.9 %copy-start.1 = (bf16[192,4096]{1,0:T(8,128)(2,1)S(1)}, bf16[192,4096]{1,0:T(8,128)(2,1)}, u32[]{:S(2)}) copy-start(bf16[192,4096]{1,0:T(8,128)(2,1)} %copy-done) | copy-start | bytes 4718596
  128.4 16.9 %copy-start.3 = (bf16[128,4096]{1,0:T(8,128)(2,1)S(1)}, bf16[128,4096]{1,0:T(8,128)(2,1)}, u32[]{:S(2)}) copy-start(bf16[128,4096]{1,0:T(8,128)(2,1)} %copy-done.2) | copy-start | bytes 3145732
  128.4 30.8 %collective-permute-start.22 = (bf16[192,2048]{1,0:T(8,128)(2,1)}, bf16[192,2048]{1,0:T(8,128)(2,1)S(1)}, u32[]{:S(2)}, u32[]{:S(2)}) collective-permute-start(bf16[192,2048]{1,0:T(8,128)(2,1)} %get-tuple-element.59), channel_id=1, source_target_pairs={{0,1},{1,0},{2,3},{3,2},{4,5},{5,4},{6,7},{7,6},{8,9},{9,8},{10,11... | collective-permute-start | bytes 2359304 | tf_op jit(solution)/shard_map/ppermute | solution.py:23
  129.1 31.8 %collective-permute-start.23 = (bf16[192,2048]{1,0:T(8,128)(2,1)}, bf16[192,2048]{1,0:T(8,128)(2,1)}, u32[]{:S(2)}, u32[]{:S(2)}) collective-permute-start(bf16[192,2048]{1,0:T(8,128)(2,1)} %get-tuple-element.60), channel_id=1, source_target_pairs={{0,2},{1,3},{2,0},{3,1},{4,6},{5,7},{6,4},{7,5},{8,10},{9,11},{10,... | collective-permute-start | bytes 2359304 | tf_op jit(solution)/shard_map/ppermute | solution.py:23
  145.2 26.8 %collective-permute-start.32 = (bf16[128,2176]{1,0:T(8,128)(2,1)S(1)}, bf16[128,2176]{1,0:T(8,128)(2,1)S(1)}, u32[]{:S(2)}, u32[]{:S(2)}) collective-permute-start(bf16[128,2176]{1,0:T(8,128)(2,1)S(1)} %get-tuple-element.61), channel_id=1, source_target_pairs={{0,4},{1,5},{2,6},{3,7},{4,0},{5,1},{6,2},{7,3},{8,12},{9,13},{10,... | collective-permute-start | bytes 1671176 | tf_op jit(solution)/shard_map/ppermute | solution.py:23
  145.3 1.2 copy-start.5
  158.0 17.2 %collective-permute-start.33 = (bf16[192,2176]{1,0:T(8,128)(2,1)S(1)}, bf16[192,2176]{1,0:T(8,128)(2,1)S(1)}, u32[]{:S(2)}, u32[]{:S(2)}) collective-permute-start(bf16[192,2176]{1,0:T(8,128)(2,1)S(1)} %get-tuple-element.62), channel_id=1, source_target_pairs={{0,1},{1,0},{2,3},{3,2},{4,5},{5,4},{6,7},{7,6},{8,9},{9,8},{10,11... | collective-permute-start | bytes 2506760 | tf_op jit(solution)/shard_map/ppermute | solution.py:23
  159.1 0.9 copy-start.10
  160.0 3.7 %copy-start.11 = (bf16[192,2048]{1,0:T(8,128)(2,1)S(1)}, bf16[192,2048]{1,0:T(8,128)(2,1)}, u32[]{:S(2)}) copy-start(bf16[192,2048]{1,0:T(8,128)(2,1)} %copy-done.10) | copy-start | bytes 2359300
  160.0 18.0 %collective-permute-start.34 = (bf16[192,2176]{1,0:T(8,128)(2,1)S(1)}, bf16[192,2176]{1,0:T(8,128)(2,1)S(1)}, u32[]{:S(2)}, u32[]{:S(2)}) collective-permute-start(bf16[192,2176]{1,0:T(8,128)(2,1)S(1)} %get-tuple-element.63), channel_id=1, source_target_pairs={{0,2},{1,3},{2,0},{3,1},{4,6},{5,7},{6,4},{7,5},{8,10},{9,11},{10,... | collective-permute-start | bytes 2506760 | tf_op jit(solution)/shard_map/ppermute | solution.py:23
  163.0 29.8 %collective-permute-start.28 = (bf16[96,2048]{1,0:T(8,128)(2,1)}, bf16[96,2048]{1,0:T(8,128)(2,1)}, u32[]{:S(2)}, u32[]{:S(2)}) collective-permute-start(bf16[96,2048]{1,0:T(8,128)(2,1)} %get-tuple-element.82), channel_id=1, source_target_pairs={{0,1},{1,0},{2,3},{3,2},{4,5},{5,4},{6,7},{7,6},{8,9},{9,8},{10,11... | collective-permute-start | bytes 1179656 | tf_op jit(solution)/shard_map/ppermute | solution.py:23
  172.0 22.1 %collective-permute-start.26 = (bf16[96,2048]{1,0:T(8,128)(2,1)S(1)}, bf16[96,2048]{1,0:T(8,128)(2,1)S(1)}, u32[]{:S(2)}, u32[]{:S(2)}) collective-permute-start(bf16[96,2048]{1,0:T(8,128)(2,1)S(1)} %get-tuple-element.80), channel_id=1, source_target_pairs={{0,4},{1,5},{2,6},{3,7},{4,0},{5,1},{6,2},{7,3},{8,12},{9,13},{10,... | collective-permute-start | bytes 1179656 | tf_op jit(solution)/shard_map/ppermute | solution.py:23
  175.2 8.4 %collective-permute-start.24 = (bf16[64,2048]{1,0:T(8,128)(2,1)S(1)}, bf16[64,2048]{1,0:T(8,128)(2,1)S(1)}, u32[]{:S(2)}, u32[]{:S(2)}) collective-permute-start(bf16[64,2048]{1,0:T(8,128)(2,1)S(1)} %get-tuple-element.86), channel_id=1, source_target_pairs={{0,2},{1,3},{2,0},{3,1},{4,6},{5,7},{6,4},{7,5},{8,10},{9,11},{10,... | collective-permute-start | bytes 786440 | tf_op jit(solution)/shard_map/ppermute | solution.py:23
  178.2 20.6 %collective-permute-start.39 = (bf16[96,2176]{1,0:T(8,128)(2,1)S(1)}, bf16[96,2176]{1,0:T(8,128)(2,1)S(1)}, u32[]{:S(2)}, u32[]{:S(2)}) collective-permute-start(bf16[96,2176]{1,0:T(8,128)(2,1)S(1)} %get-tuple-element.78), channel_id=1, source_target_pairs={{0,1},{1,0},{2,3},{3,2},{4,5},{5,4},{6,7},{7,6},{8,9},{9,8},{10,11... | collective-permute-start | bytes 1253384 | tf_op jit(solution)/shard_map/ppermute | solution.py:23
  183.6 8.1 %collective-permute-start.35 = (bf16[64,2176]{1,0:T(8,128)(2,1)S(1)}, bf16[64,2176]{1,0:T(8,128)(2,1)S(1)}, u32[]{:S(2)}, u32[]{:S(2)}) collective-permute-start(bf16[64,2176]{1,0:T(8,128)(2,1)S(1)} %get-tuple-element.84), channel_id=1, source_target_pairs={{0,2},{1,3},{2,0},{3,1},{4,6},{5,7},{6,4},{7,5},{8,10},{9,11},{10,... | collective-permute-start | bytes 835592 | tf_op jit(solution)/shard_map/ppermute | solution.py:23
  191.7 7.5 %collective-permute-start.37 = (bf16[96,2176]{1,0:T(8,128)(2,1)S(1)}, bf16[96,2176]{1,0:T(8,128)(2,1)S(1)}, u32[]{:S(2)}, u32[]{:S(2)}) collective-permute-start(bf16[96,2176]{1,0:T(8,128)(2,1)S(1)} %get-tuple-element.76), channel_id=1, source_target_pairs={{0,4},{1,5},{2,6},{3,7},{4,0},{5,1},{6,2},{7,3},{8,12},{9,13},{10,... | collective-permute-start | bytes 1253384 | tf_op jit(solution)/shard_map/ppermute | solution.py:23
  192.9 4.5 %collective-permute-start.25 = (bf16[32,2048]{1,0:T(8,128)(2,1)S(1)}, bf16[32,2048]{1,0:T(8,128)(2,1)S(1)}, u32[]{:S(2)}, u32[]{:S(2)}) collective-permute-start(bf16[32,2048]{1,0:T(8,128)(2,1)S(1)} %get-tuple-element.98), channel_id=1, source_target_pairs={{0,1},{1,0},{2,3},{3,2},{4,5},{5,4},{6,7},{7,6},{8,9},{9,8},{10,11... | collective-permute-start | bytes 393224 | tf_op jit(solution)/shard_map/ppermute | solution.py:23
  194.1 6.2 %collective-permute-start.36 = (bf16[32,2176]{1,0:T(8,128)(2,1)S(1)}, bf16[32,2176]{1,0:T(8,128)(2,1)S(1)}, u32[]{:S(2)}, u32[]{:S(2)}) collective-permute-start(bf16[32,2176]{1,0:T(8,128)(2,1)S(1)} %get-tuple-element.96), channel_id=1, source_target_pairs={{0,1},{1,0},{2,3},{3,2},{4,5},{5,4},{6,7},{7,6},{8,9},{9,8},{10,11... | collective-permute-start | bytes 417800 | tf_op jit(solution)/shard_map/ppermute | solution.py:23
  197.4 5.8 %collective-permute-start.29 = (bf16[48,2048]{1,0:T(8,128)(2,1)S(1)}, bf16[48,2048]{1,0:T(8,128)(2,1)S(1)}, u32[]{:S(2)}, u32[]{:S(2)}) collective-permute-start(bf16[48,2048]{1,0:T(8,128)(2,1)S(1)} %get-tuple-element.94), channel_id=1, source_target_pairs={{0,4},{1,5},{2,6},{3,7},{4,0},{5,1},{6,2},{7,3},{8,12},{9,13},{10,... | collective-permute-start | bytes 589832 | tf_op jit(solution)/shard_map/ppermute | solution.py:23
  198.9 4.9 %collective-permute-start.27 = (bf16[48,2048]{1,0:T(8,128)(2,1)S(1)}, bf16[48,2048]{1,0:T(8,128)(2,1)S(1)}, u32[]{:S(2)}, u32[]{:S(2)}) collective-permute-start(bf16[48,2048]{1,0:T(8,128)(2,1)S(1)} %get-tuple-element.92), channel_id=1, source_target_pairs={{0,2},{1,3},{2,0},{3,1},{4,6},{5,7},{6,4},{7,5},{8,10},{9,11},{10,... | collective-permute-start | bytes 589832 | tf_op jit(solution)/shard_map/ppermute | solution.py:23
  199.2 17.1 %collective-permute-start.40 = (bf16[48,2176]{1,0:T(8,128)(2,1)S(1)}, bf16[48,2176]{1,0:T(8,128)(2,1)S(1)}, u32[]{:S(2)}, u32[]{:S(2)}) collective-permute-start(bf16[48,2176]{1,0:T(8,128)(2,1)S(1)} %get-tuple-element.90), channel_id=1, source_target_pairs={{0,4},{1,5},{2,6},{3,7},{4,0},{5,1},{6,2},{7,3},{8,12},{9,13},{10,... | collective-permute-start | bytes 626696 | tf_op jit(solution)/shard_map/ppermute | solution.py:23
  200.3 16.1 %collective-permute-start.38 = (bf16[48,2176]{1,0:T(8,128)(2,1)S(1)}, bf16[48,2176]{1,0:T(8,128)(2,1)S(1)}, u32[]{:S(2)}, u32[]{:S(2)}) collective-permute-start(bf16[48,2176]{1,0:T(8,128)(2,1)S(1)} %get-tuple-element.88), channel_id=1, source_target_pairs={{0,2},{1,3},{2,0},{3,1},{4,6},{5,7},{6,4},{7,5},{8,10},{9,11},{10,... | collective-permute-start | bytes 626696 | tf_op jit(solution)/shard_map/ppermute | solution.py:23
  203.8 30.3 %collective-permute-start.31 = (bf16[64,2048]{1,0:T(8,128)(2,1)S(1)}, bf16[64,2048]{1,0:T(8,128)(2,1)S(1)}, u32[]{:S(2)}, u32[]{:S(2)}) collective-permute-start(bf16[64,2048]{1,0:T(8,128)(2,1)S(1)} %pad_maximum_fusion.19), channel_id=1, source_target_pairs={{0,24},{1,25},{2,26},{3,27},{4,28},{5,29},{6,30},{7,31},{8,16},{9,... | collective-permute-start | bytes 786440 | tf_op jit(solution)/shard_map/ppermute | solution.py:85
  216.2 17.9 %collective-permute-start.30 = (bf16[64,2048]{1,0:T(8,128)(2,1)S(1)}, bf16[64,2048]{1,0:T(8,128)(2,1)S(1)}, u32[]{:S(2)}, u32[]{:S(2)}) collective-permute-start(bf16[64,2048]{1,0:T(8,128)(2,1)S(1)} %pad_maximum_fusion.18), channel_id=1, source_target_pairs={{0,16},{1,17},{2,18},{3,19},{4,20},{5,21},{6,22},{7,23},{8,24},{9,... | collective-permute-start | bytes 786440 | tf_op jit(solution)/shard_map/ppermute | solution.py:86
  216.5 21.8 %collective-permute-start.42 = (bf16[64,2176]{1,0:T(8,128)(2,1)S(1)}, bf16[64,2176]{1,0:T(8,128)(2,1)S(1)}, u32[]{:S(2)}, u32[]{:S(2)}) collective-permute-start(bf16[64,2176]{1,0:T(8,128)(2,1)S(1)} %pad_maximum_fusion.16), channel_id=1, source_target_pairs={{0,24},{1,25},{2,26},{3,27},{4,28},{5,29},{6,30},{7,31},{8,16},{9,... | collective-permute-start | bytes 835592 | tf_op jit(solution)/shard_map/ppermute | solution.py:85
  221.8 16.5 %collective-permute-start.41 = (bf16[64,2176]{1,0:T(8,128)(2,1)S(1)}, bf16[64,2176]{1,0:T(8,128)(2,1)S(1)}, u32[]{:S(2)}, u32[]{:S(2)}) collective-permute-start(bf16[64,2176]{1,0:T(8,128)(2,1)S(1)} %pad_maximum_fusion.15), channel_id=1, source_target_pairs={{0,16},{1,17},{2,18},{3,19},{4,20},{5,21},{6,22},{7,23},{8,24},{9,... | collective-permute-start | bytes 835592 | tf_op jit(solution)/shard_map/ppermute | solution.py:86
